TPU v7x, 128 devices: a whole 4x4x4 slice. The times are simulated.
128 devices in a mesh: blk: 8 (over z, core), grp: 16 (over x, y).
Axes of the slice: x: 4, y: 4, z: 4, core: 2. Of those that a mesh axis runs over, the one named last changes fastest.
Arguments:
- user_prior: float32 [32768, 128], P(('blk', 'grp')), may hold values from -6 to 6
- item_factors: bfloat16 [524288, 128], P(('blk', 'grp')), may hold values from -0.375 to 0.375
- user_tiles: int32 [8192], P(('blk', 'grp')), may hold values from 0 to 31
- item_tiles: int32 [8192], P(('blk', 'grp')), may hold values from 0 to 4095, as said below
- counts: int32 [8192, 128, 128], P(('blk', 'grp')), may hold values from 0 to 20, as said below
Outputs:
- user_factors: float32 [32768, 128], P(('blk', 'grp'))
Inputs may be any that keep to these rules, and one draw needn't show every extreme that they name: `item_tiles`: item tile t is held by device t // 32 of blk+grp. The entries of one device name tiles of 32 different holders, exactly 2 entries for each holder that they name, in no particular order. In each device's 64 entries, those whose tile of counts has a nonzero value come before those whose tile is all zero; in every group along grp at least one device has all 64 entries of the first kind.
All inputs are finite; a program needn't handle non-finite values.
Results may differ from a plain program's by a relative error of at most 0.0003.
The roundings to bfloat16 on the way count: a program that leaves them out, or rounds other values in their place, can miss the bound.
Values may be sent and summed in bfloat16 or wider, within the bound.
A program may use at most 128 MiB of HBM per device.

v0:
```python
import jax
import jax.numpy as jnp
from jax import lax
from jax.sharding import PartitionSpec as P

ITERS = 3


ALPHA = 40.0
REG = 32.0
EPS = 1e-06


def fetch_tiles(item_factors, item_tiles, pairs, tile, rank):
    n_all = lax.axis_size(("blk", "grp"))
    tiles_held = item_factors.shape[0] // tile
    slots_each = max(2, pairs // n_all)
    owner = item_tiles // tiles_held
    local_slot = item_tiles % tiles_held
    position = jnp.arange(pairs, dtype=jnp.int32)
    earlier = (owner[None, :] == owner[:, None]) & (position[None, :] < position[:, None])
    order = jnp.sum(earlier.astype(jnp.int32), axis=1)
    requests = jnp.full((n_all, slots_each), -1, jnp.int32).at[owner, order].set(local_slot)
    wanted = lax.all_to_all(requests, ("blk", "grp"), split_axis=0, concat_axis=0, tiled=True)
    held = item_factors.reshape(tiles_held, tile, rank)
    picked = jnp.take(held, jnp.maximum(wanted, 0), axis=0)
    picked = jnp.where((wanted >= 0)[:, :, None, None], picked, jnp.zeros((), picked.dtype))
    arrived = lax.all_to_all(picked, ("blk", "grp"), split_axis=0, concat_axis=0, tiled=True)
    return arrived[owner, order]


def body(user_prior, item_factors, user_tiles, item_tiles, counts):
    pairs = counts.shape[0]
    tile = counts.shape[1]
    rank = item_factors.shape[1]
    n_grp = lax.axis_size("grp")
    own_rows = user_prior.shape[0]
    block_rows = own_rows * n_grp
    user_blocks = block_rows // tile
    span = min(32, pairs)
    gram_local = lax.dot_general(
        item_factors, item_factors, (((0,), (0,)), ((), ())), preferred_element_type=jnp.float32
    )
    gram = lax.psum(gram_local, ("blk", "grp"))
    pair_tiles = fetch_tiles(item_factors, item_tiles, pairs, tile, rank)
    live = jnp.sum(jnp.any(counts > 0, axis=(1, 2)).astype(jnp.int32))
    rounds = (live + span - 1) // span
    tile_ids = jnp.arange(user_blocks, dtype=jnp.int32)

    def accumulate(low_tiles, with_rhs):

        def one_round(index, totals):
            start = index * span
            users = lax.dynamic_slice_in_dim(user_tiles, start, span)
            factors = lax.dynamic_slice_in_dim(pair_tiles, start, span)
            counted = lax.dynamic_slice_in_dim(counts, start, span).astype(jnp.float32)
            selector = (tile_ids[:, None] == users[None, :]).astype(jnp.float32)
            users_low = jnp.take(low_tiles, users, axis=0)
            scores = jnp.einsum(
                "bur,bir->bui", users_low, factors, preferred_element_type=jnp.float32
            )
            scaled = (ALPHA * counted * scores).astype(jnp.bfloat16)
            back = jnp.einsum("bui,bir->bur", scaled, factors, preferred_element_type=jnp.float32)
            result = [
                totals[0]
                + jnp.einsum("tb,bur->tur", selector, back, precision=lax.Precision.HIGHEST)
            ]
            if with_rhs:
                confidence = jnp.where(counted > 0, 1.0 + ALPHA * counted, 0.0).astype(jnp.bfloat16)
                pulled = jnp.einsum(
                    "bui,bir->bur", confidence, factors, preferred_element_type=jnp.float32
                )
                result.append(
                    totals[1]
                    + jnp.einsum("tb,bur->tur", selector, pulled, precision=lax.Precision.HIGHEST)
                )
            return tuple(result)

        zeros = jnp.zeros((user_blocks, tile, rank), jnp.float32)
        start_state = (zeros, zeros) if with_rhs else (zeros,)
        totals = lax.fori_loop(0, rounds, one_round, start_state)
        return tuple((total.reshape(block_rows, rank) for total in totals))

    def gram_term(vectors):
        return jnp.dot(vectors, gram, precision=lax.Precision.HIGHEST) + REG * vectors

    def row_sum(left, right):
        return jnp.sum(left * right, axis=1, keepdims=True)

    whole = lax.all_gather(user_prior, "grp", axis=0, tiled=True)
    pair_part, rhs_part = accumulate(
        whole.astype(jnp.bfloat16).reshape(user_blocks, tile, rank), True
    )
    pair_total, rhs_total = lax.psum((pair_part, rhs_part), "grp")
    solution = whole
    residual = rhs_total - (gram_term(solution) + pair_total)
    direction = residual
    norm_now = row_sum(residual, residual)
    for step in range(ITERS):
        (pair_part,) = accumulate(
            direction.astype(jnp.bfloat16).reshape(user_blocks, tile, rank), False
        )
        image = gram_term(direction) + lax.psum(pair_part, "grp")
        alpha = norm_now / (row_sum(direction, image) + EPS)
        solution = solution + alpha * direction
        residual = residual - alpha * image
        fresh = row_sum(residual, residual)
        direction = residual + fresh / (norm_now + EPS) * direction
        norm_now = fresh
    return lax.dynamic_slice_in_dim(solution, lax.axis_index("grp") * own_rows, own_rows, 0)


def solution(mesh):
    in_specs = (
        P(("blk", "grp"), None),
        P(("blk", "grp"), None),
        P(("blk", "grp")),
        P(("blk", "grp")),
        P(("blk", "grp"), None, None),
    )
    out_specs = P(("blk", "grp"), None)
    return jax.shard_map(body, mesh=mesh, in_specs=in_specs, out_specs=out_specs, check_vma=False)
```

profile of v0, /device:TPU:0, one launch (start us, length us, event | category | flops | bytes accessed | tf_op | source)
XLA Modules:
  0.0 786.6 jit_solution(2010041510047153230)
XLA Ops:
  15.4 20.5 %all_to_all.14 = s32[128,1,2]{2,1,0:T(1,128)S(1)} all-to-all(s32[128,1,2]{2,1,0:T(1,128)S(1)} %copy.108), channel_id=1, replica_groups=mesh['blk'=8,'grp'=16] {'blk','grp'}, dimensions={0} | all-to-all | bytes 2048 | tf_op jit(solution)/shard_map/all_to_all | solution.py:24
  36.5 8.3 %gather_fusion.4 = bf16[256,128,128]{2,1,0:T(8,128)(2,1)} fusion(bf16[32,128,128]{2,1,0:T(8,128)(2,1)S(1)} %bitcast.108, s32[1024]{0:T(1024)S(1)} %pad_clamp_fusion.4), kind=kCustom, calls=%fused_computation.4 | custom fusion | bytes 16778240 | tf_op jit(solution)/shard_map/jit(_take)/gather | solution.py:26
  44.9 7.4 select_select_fusion
  52.3 6.1 all-to-all-start.1
  61.1 104.8 %all-gather.2.cloned.1.call-done = f32[4096,128]{0,1:T(8,128)} async-done(((f32[256,128]{0,1:T(8,128)}), f32[4096,128]{0,1:T(8,128)}) %all-gather.2.cloned.1.call-update) | async-done | bytes 2097168 | tf_op jit(solution)/shard_map/all_gather | solution.py:90
  176.5 18.2 %while.46 = (s32[]{:T(128)}, f32[32,128,128]{2,0,1:T(8,128)}, f32[32,128,128]{2,0,1:T(8,128)}, s32[]{:T(128)}, s32[64]{0:T(128)S(1)}, /*index=5*/s32[64,128,128]...) while((s32[]{:T(128)}, f32[32,128,128]{2,0,1:T(8,128)}, ...), condition=%wide.region_5.7_spmd.clone, body=%wide.region_4.6_spmd.clone.sunk | while | flops 812125440 | bytes 44048128 | solution.py:81
  182.8 6.1 fusion.187
  189.4 5.4 fusion.189
  198.2 4.6 copy.165
  206.3 4.6 copy.166
  211.1 58.5 %all-reduce.7.cloned.1.call-done = f32[128,128]{1,0:T(8,128)} async-done(((f32[128,128]{1,0:T(8,128)}), f32[128,128]{1,0:T(8,128)}) %all-reduce.7.cloned.1.call-update) | async-done | bytes 65552 | tf_op jit(solution)/shard_map/psum | solution.py:44
  269.7 105.7 %all-reduce.15.cloned.1.call-done = (f32[4096,128]{0,1:T(8,128)}, f32[4096,128]{0,1:T(8,128)}) async-done(((f32[4096,128]{0,1:T(8,128)}, f32[4096,128]{0,1:T(8,128)}), (f32[4096,128]{0,1:T(8,128)}, f32[4096,128]{0,1:T(8,128)})) %all-reduce.15.cloned.1.call-update) | async-done | bytes 4194320 | tf_op jit(solution)/shard_map/psum | solution.py:94
  375.4 7.0 fusion.133
  385.3 12.0 %while.47 = (s32[]{:T(128)}, f32[32,128,128]{2,0,1:T(8,128)}, s32[]{:T(128)}, s32[64]{0:T(128)S(1)}, s32[64,128,128]{2,1,0:T(8,128)}, /*index=5*/bf16[32,128,128...) while((s32[]{:T(128)}, f32[32,128,128]{2,0,1:T(8,128)}, ...), condition=%wide.region_11.13_spmd.clone, body=%wide.region_10.12_spmd.clone.sunk | while | flops 472910112 | bytes 15735391 | solution.py:81
  391.5 5.9 fusion.196
  405.8 102.2 %all-reduce.9.cloned.1.call-done = f32[4096,128]{0,1:T(8,128)} async-done(((f32[4096,128]{0,1:T(8,128)}), f32[4096,128]{0,1:T(8,128)}) %all-reduce.9.cloned.1.call-update) | async-done | bytes 2097168 | tf_op jit(solution)/shard_map/psum | solution.py:103
  508.0 5.5 multiply_reduce_fusion.3
  518.9 12.1 %while.48 = (s32[]{:T(128)}, f32[32,128,128]{2,0,1:T(8,128)}, s32[]{:T(128)}, s32[64]{0:T(128)S(1)}, s32[64,128,128]{2,1,0:T(8,128)}, /*index=5*/bf16[32,128,128...) while((s32[]{:T(128)}, f32[32,128,128]{2,0,1:T(8,128)}, ...), condition=%wide.region_16.18_spmd.clone, body=%wide.region_15.17_spmd.clone.sunk | while | flops 472910112 | bytes 15735391 | solution.py:81
  525.1 5.9 fusion.203
  539.3 101.7 %all-reduce.11.cloned.1.call-done = f32[4096,128]{0,1:T(8,128)} async-done(((f32[4096,128]{0,1:T(8,128)}), f32[4096,128]{0,1:T(8,128)}) %all-reduce.11.cloned.1.call-update) | async-done | bytes 2097168 | tf_op jit(solution)/shard_map/psum | solution.py:103
  640.9 5.3 multiply_reduce_fusion.1
  652.6 12.3 %while.49 = (s32[]{:T(128)}, f32[32,128,128]{2,0,1:T(8,128)}, s32[]{:T(128)}, s32[64]{0:T(128)S(1)}, s32[64,128,128]{2,1,0:T(8,128)}, /*index=5*/bf16[32,128,128...) while((s32[]{:T(128)}, f32[32,128,128]{2,0,1:T(8,128)}, ...), condition=%wide.region_21.23_spmd.clone, body=%wide.region_20.22_spmd.clone.sunk | while | flops 472910112 | bytes 15735391 | solution.py:81
  658.8 5.9 fusion.210
  670.8 102.3 %all-reduce.13.cloned.1.call-done = f32[4096,128]{0,1:T(8,128)} async-done(((f32[4096,128]{0,1:T(8,128)}), f32[4096,128]{0,1:T(8,128)}) %all-reduce.13.cloned.1.call-update) | async-done | bytes 2097168 | tf_op jit(solution)/shard_map/psum | solution.py:103
  (109 shorter events, 96.5 us)
Async XLA Ops:
  7.4 29.1 %copy-start = (bf16[4096,128]{1,0:T(8,128)(2,1)S(1)}, bf16[4096,128]{1,0:T(8,128)(2,1)}, u32[]{:S(2)}) copy-start(bf16[4096,128]{1,0:T(8,128)(2,1)} %param.16) | copy-start | bytes 3145732
  7.4 3.5 copy-start.11
  52.3 6.1 copy-start.10
  52.3 116.7 %all-to-all-start.1 = ((bf16[128,2,128,128]{3,2,1,0:T(8,128)(2,1)}), bf16[128,2,128,128]{3,2,1,0:T(8,128)(2,1)}, u32[]{:S(2)}, u32[]{:S(2)}) async-start(bf16[128,2,128,128]{3,2,1,0:T(8,128)(2,1)} %select_select_fusion), calls=%async_computation.1 | async-start | bytes 16777216 | tf_op jit(solution)/shard_map/all_to_all | solution.py:28
  58.3 107.5 %all-gather.2.cloned.1.call-start = ((), (), s32[]{:S(2)}) async-start(), calls=%async_computation.2 | async-start | bytes 2228224 | tf_op jit(solution)/shard_map/all_gather | solution.py:90
  59.2 210.5 %all-reduce.7.cloned.1.call-start = ((), (), s32[]{:S(2)}) async-start(), calls=%async_computation.3 | async-start | bytes 131072 | tf_op jit(solution)/shard_map/psum | solution.py:44
  60.3 315.1 %all-reduce.15.cloned.1.call-start = ((), (), s32[]{:S(2)}) async-start(), calls=%async_computation.7 | async-start | bytes 8388608 | tf_op jit(solution)/shard_map/psum | solution.py:94
  173.3 3.2 copy-start.9
  182.8 6.1 copy-start.2
  210.9 297.1 %all-reduce.9.cloned.1.call-start = ((), (), s32[]{:S(2)}) async-start(), calls=%async_computation.4 | async-start | bytes 4194304 | tf_op jit(solution)/shard_map/psum | solution.py:103
  405.3 102.7 %copy-start.8 = (f32[128,128]{1,0:T(8,128)S(1)}, f32[128,128]{1,0:T(8,128)}, u32[]{:S(2)}) copy-start(f32[128,128]{1,0:T(8,128)} %all-reduce.7.cloned.1.call-done) | copy-start | bytes 196612
  405.3 235.6 %all-reduce.11.cloned.1.call-start = ((), (), s32[]{:S(2)}) async-start(), calls=%async_computation.5 | async-start | bytes 4194304 | tf_op jit(solution)/shard_map/psum | solution.py:103
  508.0 5.5 copy-start.3
  514.0 2.0 copy-start.4
  539.0 234.1 %all-reduce.13.cloned.1.call-start = ((), (), s32[]{:S(2)}) async-start(), calls=%async_computation.6 | async-start | bytes 4194304 | tf_op jit(solution)/shard_map/psum | solution.py:103
  640.9 5.4 copy-start.5
  646.3 1.6 copy-start.6
  670.6 102.5 %copy-start.7 = (f32[4096,128]{0,1:T(8,128)S(1)}, f32[4096,128]{0,1:T(8,128)}, u32[]{:S(2)}) copy-start(f32[4096,128]{0,1:T(8,128)} %get-tuple-element.504) | copy-start | bytes 6291460
  773.1 5.9 copy-start.1
Sparse Core Ops, SparseCore 0:
  61.3 104.5 all-gather.1
  405.5 102.5 all-reduce.8
  670.8 102.2 all-reduce.12
Sparse Core Ops, SparseCore 1:
  64.4 205.2 all-reduce.6
  272.9 102.4 all-reduce.14
  539.1 101.7 all-reduce.10
where the time goes:
time: 794 us; the launch traced here: 787 us
  waiting for transfers between devices  575 us (72%)
  local copies, waits for them, and re-layouts  78.8 us (10%)
  matrix products  69 us (9%)
  blocking collectives  20.5 us (3%)
  other arithmetic  19.5 us (2%)
  between operations  16 us (2%)
    psum x3, waiting for transfers between devices, body(): image = gram_term(direction) + lax.psum(pair_part, 'grp')  306 us
    psum x1, waiting for transfers between devices, body(): pair_total, rhs_total = lax.psum((pair_part, rhs_part), 'grp')  106 us
    all_gather x1, waiting for transfers between devices, body(): whole = lax.all_gather(user_prior, 'grp', axis=0, tiled=True)  105 us
    psum x1, waiting for transfers between devices, body(): gram = lax.psum(gram_local, ('blk', 'grp'))  58.5 us
    unnamed x32, local copies, waits for them, and re-layouts  28.6 us
    dot_general x4, matrix products, one_round(): jnp.einsum('tb,bur->tur', selector, back, precision=lax.Precision.HIGHEST)  23.8 us
    dot_general x4, matrix products, gram_term(): jnp.dot(vectors, gram, precision=lax.Precision.HIGHEST) + REG * vectors  21.8 us
    all_to_all x1, blocking collectives, fetch_tiles(): lax.all_to_all(requests, ('blk', 'grp'), split_axis=0, concat_axis=0, til...  20.5 us
  transfers between devices with their start and end apart: 7, of which 6 were waited for; matrix products, arithmetic and copies ran while one was open for 6% of the time, Pallas kernels for 0%

commit v1 on v0

v1 whole, which is shorter than its diff:
```python
import functools

import jax
import jax.numpy as jnp
from jax import lax
from jax.experimental import pallas as pl
from jax.experimental.pallas import tpu as pltpu
from jax.sharding import PartitionSpec as P

ITERS = 3
ALPHA = 40.0
REG = 32.0
EPS = 1e-06
SIDE = 4
MESH = pl.DeviceIdType.MESH
STRIDE = 53


def coords():
    b = lax.axis_index("blk")
    g = lax.axis_index("grp")
    return b, g, g // SIDE, g % SIDE


def row_col(axis, k):
    b, g, x, y = coords()
    if axis == 0:
        return b, ((x + k) % SIDE) * SIDE + y
    return b, x * SIDE + (y + k) % SIDE


def remote(src, dst, send_sem, recv_sem, device):
    return pltpu.make_async_remote_copy(
        src_ref=src, dst_ref=dst, send_sem=send_sem, recv_sem=recv_sem,
        device_id=device, device_id_type=MESH,
    )


def tile_place(u):
    g = u // 2
    x, y = g // SIDE, g % SIDE
    return jnp.where(u % 2 == 0, y * SIDE + x, SIDE * SIDE + x * SIDE + y)


def gather_first(low, sems):
    _, _, x, y = coords()
    copies = []
    for k in range(1, SIDE):
        for t in range(2):
            place = y * SIDE + x if t == 0 else SIDE * SIDE + x * SIDE + y
            copies.append(remote(
                low.at[place], low.at[place], sems.at[0, 0, t, k], sems.at[0, 1, t, k],
                row_col(t, k),
            ))
    return copies


def gather_second(low, sems):
    _, _, x, y = coords()
    copies = []
    for k in range(1, SIDE):
        for t in range(2):
            start = y * SIDE if t == 0 else SIDE * SIDE + x * SIDE
            copies.append(remote(
                low.at[pl.ds(start, SIDE)], low.at[pl.ds(start, SIDE)],
                sems.at[1, 0, t, k], sems.at[1, 1, t, k], row_col(1 - t, k),
            ))
    return copies


def fetch_kernel(
    n_blk, n_grp,
    wanted_tiles, user_tiles, items, prior, counts,
    out_tiles, out_gram, out_low, out_weights, out_index,
    req, reqs, want, want_s, sel, sel_s, send, recv, low, gram_own, gram_a, gram_b, gram_c, gram_t,
    req_sems, tile_sems, low_sems, gram_sems, local_sem,
):
    n_all = n_blk * n_grp
    b, g, x, y = coords()
    me = b * n_grp + g
    pairs = out_tiles.shape[0]
    held = items.shape[0]
    tile = items.shape[1]
    rank = items.shape[2]

    def peer(step):
        shift = (step * STRIDE) % n_all
        db, dg = shift % n_blk, shift // n_blk
        dc, dz = db % 2, db // 2
        dx, dy = dg // SIDE, dg % SIDE
        nb = ((b // 2 + dz) % (n_blk // 2)) * 2 + (b % 2 + dc) % 2
        ng = ((x + dx) % SIDE) * SIDE + (y + dy) % SIDE
        return nb, ng

    barrier = pltpu.get_barrier_semaphore()

    def greet(step, carry):
        pl.semaphore_signal(barrier, inc=1, device_id=peer(step), device_id_type=MESH)
        return carry

    lax.fori_loop(1, n_all, greet, 0)

    lane = lax.broadcasted_iota(jnp.int32, (1, 128), 1)

    def ask(p, state):
        first, second, seen, order, last, before = state
        entry = wanted_tiles[p]
        owner, slot = entry // held, entry % held
        hit = lane == owner
        fresh = jnp.logical_and(hit, seen == 0)
        turn = jnp.sum(jnp.where(hit, seen, 0), axis=1, keepdims=True)
        order = jnp.where(lane == p, owner * 2 + jnp.minimum(turn, 1), order)
        first = jnp.where(fresh, slot, first)
        second = jnp.where(hit, slot, second)
        seen = jnp.where(hit, 1, seen)
        mine = lane == user_tiles[p]
        earlier = jnp.sum(jnp.where(mine, last, 0), axis=1, keepdims=True)
        before = jnp.where(lane == p, earlier, before)
        last = jnp.where(mine, p + 1, last)
        return first, second, seen, order, last, before

    zero = jnp.zeros((1, 128), jnp.int32)
    first, second, _, order, last, before = lax.fori_loop(0, pairs, ask, (zero,) * 6)
    row = lax.broadcasted_iota(jnp.int32, (8, 128), 0)
    req[...] = jnp.where(row == 0, first, jnp.where(row == 1, second, 0))
    sel[...] = jnp.where(row == 0, order, 0)
    out_index[...] = jnp.where(row == 0, before, jnp.where(row == 1, last, 0))
    reqs[me] = req[...]
    pltpu.make_async_copy(sel, sel_s, local_sem).start()
    low[y * SIDE + x] = prior[0].astype(jnp.bfloat16)
    low[SIDE * SIDE + x * SIDE + y] = prior[1].astype(jnp.bfloat16)
    pltpu.make_async_copy(sel, sel_s, local_sem).wait()

    pl.semaphore_wait(barrier, n_all - 1)

    def request(step):
        nb, ng = peer(step)
        return remote(req, reqs.at[me], req_sems.at[0, step], req_sems.at[1, step], (nb, ng))

    def send_request(step, carry):
        request(step).start()
        return carry

    lax.fori_loop(1, n_all, send_request, 0)

    gathers = gather_first(low, low_sems)
    for copy in gathers:
        copy.start()

    chunk = min(8, held)

    def gram_step(i, total):
        block = items[pl.ds(i * chunk, chunk)].reshape(chunk * tile, rank)
        return total + lax.dot_general(
            block, block, (((0,), (0,)), ((), ())), preferred_element_type=jnp.float32
        )

    gram_rows = rank // n_grp
    gram_own[...] = lax.fori_loop(
        0, held // chunk, gram_step, jnp.zeros((rank, rank), jnp.float32)
    ).reshape(n_grp, gram_rows, rank)

    def gram_first(k):
        ng = (g + k) % n_grp
        return remote(
            gram_own.at[ng], gram_a.at[k], gram_sems.at[0, 0, k], gram_sems.at[0, 1, k], (b, ng)
        )

    for k in range(1, n_grp):
        gram_first(k).start()

    def wait_request(step, carry):
        request(step).wait_send()
        request(step).wait_recv()
        return carry

    lax.fori_loop(1, n_all, wait_request, 0)

    def collect(d, total):
        mine = jnp.sum(jnp.where(lane == me, reqs[d], 0), axis=1, keepdims=True)
        return jnp.where(lane == d, mine, total)

    want[...] = lax.fori_loop(0, n_all, collect, jnp.zeros((8, 128), jnp.int32))
    pltpu.make_async_copy(want, want_s, local_sem).start()

    for k in range(1, n_grp):
        gram_first(k).wait()
    part = gram_own[g]
    for k in range(1, n_grp):
        part = part + gram_a[k]
    gram_t[0] = part
    pltpu.make_async_copy(want, want_s, local_sem).wait()

    def gram_second(k):
        return remote(
            gram_t.at[0], gram_b.at[k], gram_sems.at[1, 0, k], gram_sems.at[1, 1, k],
            ((b + k) % n_blk, g),
        )

    for k in range(1, n_blk):
        gram_second(k).start()

    for copy in gathers:
        copy.wait()
    gathers = gather_second(low, low_sems)
    for copy in gathers:
        copy.start()

    def pack(step):
        nb, ng = peer(step)
        to = nb * n_grp + ng
        send[step, 0] = items[want_s[0, to]]
        send[step, 1] = items[want_s[1, to]]

    def parcel(step):
        return remote(
            send.at[step], recv.at[me], tile_sems.at[0, step], tile_sems.at[1, step], peer(step)
        )

    def ship(step, carry):
        @pl.when(step + 1 < n_all)
        def _():
            pack(step + 1)

        parcel(step).start()
        return carry

    pack(1)
    half = n_all // 4
    lax.fori_loop(1, half, ship, 0)

    for k in range(1, n_blk):
        gram_second(k).wait()
    part = gram_t[0]
    for k in range(1, n_blk):
        part = part + gram_b[k]
    gram_t[1] = part
    gram_c[g] = part

    def gram_third(k):
        return remote(
            gram_t.at[1], gram_c.at[g], gram_sems.at[2, 0, k], gram_sems.at[2, 1, k],
            (b, (g + k) % n_grp),
        )

    lax.fori_loop(half, n_all, ship, 0)
    for k in range(1, n_grp):
        gram_third(k).start()
    recv[me, 0] = items[want_s[0, me]]
    recv[me, 1] = items[want_s[1, me]]

    def weigh(p, carry):
        out_weights[p] = (counts[p].astype(jnp.float32) * ALPHA).astype(jnp.bfloat16)
        return carry

    lax.fori_loop(0, pairs, weigh, 0)

    for copy in gathers:
        copy.wait()
    out_low[...] = low[...]
    for k in range(1, n_grp):
        gram_third(k).wait()
    out_gram[...] = gram_c[...].reshape(rank, rank)

    def wait_parcel(step, carry):
        parcel(step).wait_send()
        parcel(step).wait_recv()
        return carry

    lax.fori_loop(1, n_all, wait_parcel, 0)

    def take(p, carry):
        place = sel_s[0, p]
        out_tiles[p] = recv[place // 2, place % 2]
        return carry

    lax.fori_loop(0, pairs, take, 0)


def sweep_kernel(
    user_tiles, index, tiles, gram, low_in, weights, prior,
    out,
    chain, low, parts, first_in, sums, second_in, residual, direction,
    low_sems, sum_sems,
):
    pairs, tile, rank = tiles.shape
    _, _, x, y = coords()
    users = SIDE * SIDE * 2

    barrier = pltpu.get_barrier_semaphore()
    for k in range(1, SIDE):
        for axis in range(2):
            pl.semaphore_signal(barrier, inc=1, device_id=row_col(axis, k), device_id_type=MESH)

    chain[0] = jnp.zeros((tile, rank), jnp.float32)
    low[...] = low_in[...]

    def accumulate(with_rhs):
        group = 4

        def several(i, carry):
            backs = []
            for j in range(group):
                p = i * group + j
                factors = tiles[p]
                weight = weights[p].astype(jnp.float32)
                scores = lax.dot_general(
                    low[tile_place(user_tiles[p])], factors, (((1,), (1,)), ((), ())),
                    preferred_element_type=jnp.float32,
                )
                scaled = (weight * scores).astype(jnp.bfloat16)
                back = jnp.dot(scaled, factors, preferred_element_type=jnp.float32)
                if with_rhs:
                    confidence = jnp.where(weight > 0, 1.0 + weight, 0.0).astype(jnp.bfloat16)
                    back = jnp.dot(
                        confidence, factors, preferred_element_type=jnp.float32
                    ) - back
                backs.append(back)
            for j in range(group):
                p = i * group + j
                chain[p + 1] = chain[index[0, p]] + backs[j]
            return carry

        lax.fori_loop(0, pairs // group, several, 0)

        def final(u, carry):
            parts[tile_place(u)] = chain[index[1, u]]
            return carry

        lax.fori_loop(0, users, final, 0)

    def sum_first(k, t):
        away = (y + k) % SIDE if t == 0 else (x + k) % SIDE
        return remote(
            parts.at[pl.ds(t * SIDE * SIDE + away * SIDE, SIDE)], first_in.at[t, k],
            sum_sems.at[0, 0, t, k], sum_sems.at[0, 1, t, k], row_col(1 - t, k),
        )

    def sum_second(k, t):
        away = (x + k) % SIDE if t == 0 else (y + k) % SIDE
        return remote(
            sums.at[t, away], second_in.at[t, k],
            sum_sems.at[1, 0, t, k], sum_sems.at[1, 1, t, k], row_col(t, k),
        )

    def reduce_start():
        for k in range(1, SIDE):
            for t in range(2):
                sum_first(k, t).start()

    def reduce_finish():
        for k in range(1, SIDE):
            for t in range(2):
                sum_first(k, t).wait()
        for t in range(2):
            near = y if t == 0 else x
            for j in range(SIDE):
                total = parts[t * SIDE * SIDE + near * SIDE + j]
                for k in range(1, SIDE):
                    total = total + first_in[t, k, j]
                sums[t, j] = total
        for k in range(1, SIDE):
            for t in range(2):
                sum_second(k, t).start()
        for k in range(1, SIDE):
            for t in range(2):
                sum_second(k, t).wait()
        totals = []
        for t in range(2):
            total = sums[t, x if t == 0 else y]
            for k in range(1, SIDE):
                total = total + second_in[t, k]
            totals.append(total)
        return jnp.concatenate(totals, axis=0)

    def gram_term(vectors):
        return (
            jnp.dot(vectors, gram[...], precision=lax.Precision.HIGHEST,
                    preferred_element_type=jnp.float32)
            + REG * vectors
        )

    def row_sum(left, right):
        return jnp.sum(left * right, axis=1, keepdims=True)

    accumulate(True)
    pl.semaphore_wait(barrier, 2 * (SIDE - 1))
    reduce_start()
    local = gram_term(prior[...])
    start = reduce_finish() - local
    residual[...] = start
    direction[...] = start
    out[...] = prior[...]

    def iterate(step, norm_now):
        d = direction[...]
        d_low = d.astype(jnp.bfloat16)
        low[y * SIDE + x] = d_low[:tile]
        low[SIDE * SIDE + x * SIDE + y] = d_low[tile:]
        copies = gather_first(low, low_sems)
        for copy in copies:
            copy.start()
        for copy in copies:
            copy.wait()
        copies = gather_second(low, low_sems)
        for copy in copies:
            copy.start()
        for copy in copies:
            copy.wait()
        accumulate(False)
        reduce_start()
        local = gram_term(direction[...])
        image = local + reduce_finish()
        d = direction[...]
        alpha = norm_now / (row_sum(d, image) + EPS)
        out[...] = out[...] + alpha * d
        r = residual[...] - alpha * image
        residual[...] = r
        fresh = row_sum(r, r)
        direction[...] = r + fresh / (norm_now + EPS) * d
        return fresh

    lax.fori_loop(0, ITERS, iterate, row_sum(start, start))


def body(user_prior, item_factors, user_tiles, item_tiles, counts):
    n_blk = lax.axis_size("blk")
    n_grp = lax.axis_size("grp")
    n_all = n_blk * n_grp
    pairs, tile, _ = counts.shape
    rank = item_factors.shape[1]
    users = 2 * n_grp
    own = user_prior.shape[0]
    held = item_factors.shape[0] // tile
    vmem = pl.BlockSpec(memory_space=pltpu.VMEM)
    smem = pl.BlockSpec(memory_space=pltpu.SMEM)
    dma = pltpu.SemaphoreType.DMA
    items = item_factors.reshape(held, tile, rank)
    prior = user_prior.reshape(2, tile, rank)
    tiles, gram, low, weights, index = pl.pallas_call(
        functools.partial(fetch_kernel, n_blk, n_grp),
        out_shape=(
            jax.ShapeDtypeStruct((pairs, tile, rank), jnp.bfloat16),
            jax.ShapeDtypeStruct((rank, rank), jnp.float32),
            jax.ShapeDtypeStruct((users, tile, rank), jnp.bfloat16),
            jax.ShapeDtypeStruct((pairs, tile, tile), jnp.bfloat16),
            jax.ShapeDtypeStruct((8, 128), jnp.int32),
        ),
        in_specs=[smem, smem, vmem, vmem, vmem],
        out_specs=(vmem,) * 5,
        scratch_shapes=[
            pltpu.VMEM((8, 128), jnp.int32),
            pltpu.VMEM((n_all, 8, 128), jnp.int32),
            pltpu.VMEM((8, 128), jnp.int32),
            pltpu.SMEM((8, 128), jnp.int32),
            pltpu.VMEM((8, 128), jnp.int32),
            pltpu.SMEM((8, 128), jnp.int32),
            pltpu.VMEM((n_all, 2, tile, rank), jnp.bfloat16),
            pltpu.VMEM((n_all, 2, tile, rank), jnp.bfloat16),
            pltpu.VMEM((users, tile, rank), jnp.bfloat16),
            pltpu.VMEM((n_grp, rank // n_grp, rank), jnp.float32),
            pltpu.VMEM((n_grp, rank // n_grp, rank), jnp.float32),
            pltpu.VMEM((n_blk, rank // n_grp, rank), jnp.float32),
            pltpu.VMEM((n_grp, rank // n_grp, rank), jnp.float32),
            pltpu.VMEM((2, rank // n_grp, rank), jnp.float32),
            dma((2, n_all)),
            dma((2, n_all)),
            dma((2, 2, 2, SIDE)),
            dma((3, 2, n_grp)),
            dma,
        ],
        compiler_params=pltpu.CompilerParams(
            collective_id=0, has_side_effects=True, vmem_limit_bytes=60 << 20
        ),
        name="fetch",
    )(item_tiles, user_tiles, items, prior, counts)

    return pl.pallas_call(
        sweep_kernel,
        out_shape=jax.ShapeDtypeStruct((own, rank), jnp.float32),
        in_specs=[smem, smem, vmem, vmem, vmem, vmem, vmem],
        out_specs=vmem,
        scratch_shapes=[
            pltpu.VMEM((pairs + 1, tile, rank), jnp.float32),
            pltpu.VMEM((users, tile, rank), jnp.bfloat16),
            pltpu.VMEM((users, tile, rank), jnp.float32),
            pltpu.VMEM((2, SIDE, SIDE, tile, rank), jnp.float32),
            pltpu.VMEM((2, SIDE, tile, rank), jnp.float32),
            pltpu.VMEM((2, SIDE, tile, rank), jnp.float32),
            pltpu.VMEM((own, rank), jnp.float32),
            pltpu.VMEM((own, rank), jnp.float32),
            dma((2, 2, 2, SIDE)),
            dma((2, 2, 2, SIDE)),
        ],
        compiler_params=pltpu.CompilerParams(
            collective_id=1, has_side_effects=True, vmem_limit_bytes=60 << 20
        ),
        name="sweep",
    )(user_tiles, index, tiles, gram, low, weights, user_prior)


def solution(mesh):
    in_specs = (
        P(("blk", "grp"), None),
        P(("blk", "grp"), None),
        P(("blk", "grp")),
        P(("blk", "grp")),
        P(("blk", "grp"), None, None),
    )
    out_specs = P(("blk", "grp"), None)
    return jax.shard_map(body, mesh=mesh, in_specs=in_specs, out_specs=out_specs, check_vma=False)
```

time: 794 us -> 325 us (0.41)
  waiting for transfers between devices: 575 us -> 0 us
  Pallas kernels: 0 us -> 323 us
  local copies, waits for them, and re-layouts: 78.8 us -> 1.57 us
  matrix products: 69 us -> 0 us
  blocking collectives: 20.5 us -> 0 us
  other arithmetic: 19.5 us -> 0 us
  between operations: 16 us -> 0.02 us
    psum x5 -> x0, waiting for transfers between devices: 470 us -> none  [the longest x3 306 us: body(): image = gram_term(direction) + lax.psum(pair_part, 'grp')]
    pallas_call x0 -> x2, Pallas kernels: none -> 323 us  [the longest x1 172 us: body(): pl.pallas_call(functools.partial(fetch_kernel, n_blk, n_grp), out_shape=(...]
    all_gather x1 -> x0, waiting for transfers between devices: 105 us -> none  [body(): whole = lax.all_gather(user_prior, 'grp', axis=0, tiled=True)]
    dot_general x15 -> x0, matrix products: 69 us -> none  [the longest x4 23.8 us: one_round(): jnp.einsum('tb,bur->tur', selector, back, precision=lax.Precision.HIGHEST)]
    unnamed x32 -> x1, local copies, waits for them, and re-layouts: 28.6 us -> 1.57 us
    gather x6 -> x0, local copies, waits for them, and re-layouts: 20.6 us -> none  [the longest x1 8.34 us: fetch_tiles(): picked = jnp.take(held, jnp.maximum(wanted, 0), axis=0)]
    all_to_all x1 -> x0, blocking collectives: 20.5 us -> none  [fetch_tiles(): lax.all_to_all(requests, ('blk', 'grp'), split_axis=0, concat_axis=0, til...]
    while x7 -> x0, local copies, waits for them, and re-layouts: 16.5 us -> none  [the longest x5 16.5 us: accumulate(): totals = lax.fori_loop(0, rounds, one_round, start_state)]
  transfers between devices with their start and end apart: 7 -> 0, of which waited for: 6 -> 0; matrix products, arithmetic and copies ran while one was open for 6% -> 0% of each run, Pallas kernels for 0% -> 0%
where the time goes in v1:
time: 325 us
  Pallas kernels  323 us (99%)
    pallas_call x1, Pallas kernels, body(): pl.pallas_call(functools.partial(fetch_kernel, n_blk, n_grp), out_shape=(...  172 us
    pallas_call x1, Pallas kernels, body(): pl.pallas_call(sweep_kernel, out_shape=jax.ShapeDtypeStruct((own, rank),...  151 us

profile of v1, /device:TPU:0, one launch (start us, length us, event | category | flops | bytes accessed | tf_op | source)
XLA Modules:
  0.0 324.5 jit_solution(6939743001101607651)
XLA Ops:
  0.0 171.8 %fetch.1 = (bf16[64,128,128]{2,1,0:T(8,128)(2,1)}, f32[128,128]{1,0:T(8,128)}, bf16[32,128,128]{2,1,0:T(8,128)(2,1)}, bf16[64,128,128]{2,1,0:T(8,128)(2,1)}, s32[8,128]{1,0:T(8,128)}) custom-call(s32[64]{0:T(128)} %wanted_tiles.1, s32[64]{0:T(128)} %user_tiles.3, bf16[32,128,128]{2,1,0:T(8,128)(2,1)} %bitcast.2, f32[2,128,128]{2,1,0:T(8,128)} %bitcast.3, ...), custom_call_target="tpu_custom_call" | custom-call | tf_op jit(solution)/shard_map/fetch/pallas_call | solution.py:440
  171.8 151.2 %sweep.1 = f32[256,128]{1,0:T(8,128)} custom-call(s32[64]{0:T(128)} %user_tiles.3, s32[8,128]{1,0:T(8,128)} %get-tuple-element.10.index, bf16[64,128,128]{2,1,0:T(8,128)(2,1)} %get-tuple-element.11.tiles, f32[128,128]{1,0:T(8,128)} %get-tuple-element.12.gram, bf16[32,128,128]{2,1,0:T(8,128)(2,1)} %get-tuple-element.13.low_in, ...), custom_call_target="tpu_custom_call" | custom-call | tf_op jit(solution)/shard_map/sweep/pallas_call | solution.py:478
  323.0 1.6 copy.7

commit v2 on v0

v2 whole, which is shorter than its diff:
```python
import functools

import jax
import jax.numpy as jnp
from jax import lax
from jax.experimental import pallas as pl
from jax.experimental.pallas import tpu as pltpu
from jax.sharding import PartitionSpec as P

ITERS = 3
ALPHA = 40.0
REG = 32.0
EPS = 1e-06
SIDE = 4
PLANE = SIDE * SIDE
FACE = 2 * PLANE
LEVELS = 32700.0
SHARE = ((0, 48), (48, 48), (96, 32))
MESH = pl.DeviceIdType.MESH


def position():
    b = lax.axis_index("blk")
    g = lax.axis_index("grp")
    return (g // SIDE, g % SIDE, b // 2), b % 2


def mesh_id(place, core):
    x, y, z = place
    return z * 2 + core, x * SIDE + y


def flat_id(place, core):
    b, g = mesh_id(place, core)
    return b * PLANE + g


def moved(place, axis, k):
    return tuple((v + k) % SIDE if i == axis else v for i, v in enumerate(place))


def put_at(place, axis, value):
    return tuple(value if i == axis else v for i, v in enumerate(place))


def remote(src, dst, send_sem, recv_sem, device):
    return pltpu.make_async_remote_copy(
        src_ref=src, dst_ref=dst, send_sem=send_sem, recv_sem=recv_sem,
        device_id=device, device_id_type=MESH,
    )


def quantize(value):
    top = jnp.maximum(jnp.max(jnp.abs(value), axis=0, keepdims=True), 1e-30)
    whole = jnp.round(value * (LEVELS / top)).astype(jnp.int32).astype(jnp.int16)
    return whole, top * (1.0 / LEVELS)


def restore(whole, unit):
    return whole.astype(jnp.int32).astype(jnp.float32) * unit


def tile_place(u):
    g = u // 2
    x, y = g // SIDE, g % SIDE
    return jnp.where(u % 2 == 0, y * SIDE + x, PLANE + x * SIDE + y)


def kernel(
    n_blk, n_grp,
    wanted_tiles, user_tiles, items, prior, counts,
    out,
    req, reqs, want, table, table_s,
    ring0, ring1, ring2, send0, send1, send2, recv0, recv1, recv2,
    tiles, counted, weights, low, chain,
    gram_own, gram_a, gram_b, gram_c, gram_t,
    part_q, part_u, first_q, first_u, sum_q, sum_u, second_q, second_u, sums,
    residual, direction, local,
    req_sems, ring_sems, tile_sems, gather_one, gather_two, first_sems, second_sems,
    gram_sems, local_sems,
):
    n_all = n_blk * n_grp
    place, core = position()
    x, y, z = place
    b, g = mesh_id(place, core)
    me = b * n_grp + g
    pairs, tile, rank = tiles.shape
    held = items.shape[0]
    rings, sends, recvs = (ring0, ring1, ring2), (send0, send1, send2), (recv0, recv1, recv2)

    count_copy = pltpu.make_async_copy(counts, counted, local_sems.at[0])
    count_copy.start()

    def other(step):
        b_to = (b + step // n_grp) % n_blk
        return b_to, (g + step % n_grp) % n_grp

    barrier = pltpu.get_barrier_semaphore()

    def greet(step, carry):
        pl.semaphore_signal(barrier, inc=1, device_id=other(step), device_id_type=MESH)
        return carry

    lax.fori_loop(1, n_all, greet, 0)

    lane = lax.broadcasted_iota(jnp.int32, (1, 128), 1)
    zero = jnp.zeros((1, 128), jnp.int32)

    def ask(i, state):
        first, second = state
        for j in range(8):
            p = i * 8 + j
            late, early = wanted_tiles[p], wanted_tiles[pairs - 1 - p]
            second = jnp.where(lane == late // held, late % held, second)
            first = jnp.where(lane == early // held, early % held, first)
        return first, second

    first, second = lax.fori_loop(0, pairs // 8, ask, (zero, zero))
    asked = first + 256 * second
    req[...] = asked
    reqs[me] = asked
    low[y * SIDE + x] = prior[:tile].astype(jnp.bfloat16)
    low[PLANE + x * SIDE + y] = prior[tile:].astype(jnp.bfloat16)

    def keep(i, carry):
        for axis, (start, rows) in enumerate(SHARE):
            rings[axis][place[axis], i] = items[i, start:start + rows]
        return carry

    lax.fori_loop(0, held, keep, 0)

    pl.semaphore_wait(barrier, n_all - 1)

    def request(step):
        return remote(
            req, reqs.at[me], req_sems.at[0, step], req_sems.at[1, step], other(step)
        )

    def send_request(step, carry):
        request(step).start()
        return carry

    lax.fori_loop(1, n_all, send_request, 0)

    def ring_copy(axis, kind):
        start, rows = SHARE[axis]
        ring = rings[axis]
        here = place[axis]
        if kind < 2:
            src, dst = items.at[:, pl.ds(start, rows)], ring.at[here]
        else:
            origin = (here + SIDE - 1) % SIDE if kind == 2 else (here + 1) % SIDE
            half = pl.ds(0 if kind == 2 else held // 2, held // 2)
            src = dst = ring.at[origin, half]
        to = moved(place, axis, 1 if kind % 2 == 0 else SIDE - 1)
        return remote(
            src, dst, ring_sems.at[0, axis, kind], ring_sems.at[1, axis, kind],
            mesh_id(to, core),
        )

    for kind in range(2):
        for axis in range(3):
            ring_copy(axis, kind).start()

    def low_place(t, m):
        if t == 0:
            return y * SIDE + (x + SIDE - m) % SIDE
        return PLANE + x * SIDE + (y + SIDE - m) % SIDE

    def gather_a(t, k):
        ref = low.at[low_place(t, 0)]
        return remote(
            ref, ref, gather_one.at[0, t, k], gather_one.at[1, t, k],
            mesh_id(moved(place, t, k), core),
        )

    def gather_b(t, k, m):
        ref = low.at[low_place(t, m)]
        return remote(
            ref, ref, gather_two.at[0, t, k, m], gather_two.at[1, t, k, m],
            mesh_id(moved(place, 1 - t, k), core),
        )

    def gather_begin():
        for k in range(1, SIDE):
            for t in range(2):
                gather_a(t, k).start()
        for k in range(1, SIDE):
            for t in range(2):
                gather_b(t, k, 0).start()

    def gather_onward():
        for m in range(1, SIDE):
            for t in range(2):
                gather_a(t, m).wait()
                for k in range(1, SIDE):
                    gather_b(t, k, m).start()

    def gather_end():
        for m in range(SIDE):
            for k in range(1, SIDE):
                for t in range(2):
                    gather_b(t, k, m).wait()

    gather_begin()

    chunk = min(8, held)

    def gram_step(i, total):
        block = items[pl.ds(i * chunk, chunk)].reshape(chunk * tile, rank)
        return total + lax.dot_general(
            block, block, (((0,), (0,)), ((), ())), preferred_element_type=jnp.float32
        )

    gram_own[...] = lax.fori_loop(
        0, held // chunk, gram_step, jnp.zeros((rank, rank), jnp.float32)
    ).reshape(n_grp, rank // n_grp, rank)

    def gram_first(k):
        to = (g + k) % n_grp
        return remote(
            gram_own.at[to], gram_a.at[k], gram_sems.at[0, 0, k], gram_sems.at[0, 1, k], (b, to)
        )

    def gram_second(k):
        return remote(
            gram_t.at[0], gram_b.at[k], gram_sems.at[1, 0, k], gram_sems.at[1, 1, k],
            ((b + k) % n_blk, g),
        )

    def gram_third(k):
        return remote(
            gram_t.at[1], gram_c.at[g], gram_sems.at[2, 0, k], gram_sems.at[2, 1, k],
            (b, (g + k) % n_grp),
        )

    for k in range(1, n_grp):
        gram_first(k).start()

    for axis in range(3):
        for kind in range(2):
            ring_copy(axis, kind).wait()
            ring_copy(axis, kind + 2).start()

    gather_onward()

    def wait_request(step, carry):
        request(step).wait()
        return carry

    lax.fori_loop(1, n_all, wait_request, 0)
    want_copy = pltpu.make_async_copy(reqs, want, local_sems.at[1])
    want_copy.start()
    for k in range(1, n_grp):
        gram_first(k).wait()
    part = gram_own[g]
    for k in range(1, n_grp):
        part = part + gram_a[k]
    gram_t[0] = part
    want_copy.wait()
    for k in range(1, n_blk):
        gram_second(k).start()
    for axis in range(3):
        for kind in range(2, 4):
            ring_copy(axis, kind).wait()

    def face_target(axis, step):
        a, c = step // 2 // SIDE, step // 2 % SIDE
        to = moved(moved(place, (axis + 1) % 3, a), (axis + 2) % 3, c)
        return to, (core + step) % 2

    def face_index(axis):
        return (place[(axis + 1) % 3] * SIDE + place[(axis + 2) % 3]) * 2 + core

    def pack_into(ref, slot, axis, to):
        for w in range(SIDE):
            pair = want[to, 0, flat_id(put_at(place, axis, w), core)]
            ref[slot, w, 0] = rings[axis][w, pair % 256]
            ref[slot, w, 1] = rings[axis][w, pair // 256]

    def pack(step):
        for axis in range(3):
            to, to_core = face_target(axis, step)
            pack_into(sends[axis], step, axis, flat_id(to, to_core))

    def parcel(axis, step):
        to, to_core = face_target(axis, step)
        return remote(
            sends[axis].at[step], recvs[axis].at[face_index(axis)],
            tile_sems.at[0, axis, step], tile_sems.at[1, axis, step], mesh_id(to, to_core),
        )

    def ship(step, carry):
        pack(step + 1)
        for axis in range(3):
            parcel(axis, step).start()
        return carry

    pack(1)
    lax.fori_loop(1, FACE // 4, ship, 0)
    for k in range(1, n_blk):
        gram_second(k).wait()
    part = gram_t[0]
    for k in range(1, n_blk):
        part = part + gram_b[k]
    gram_t[1] = part
    gram_c[g] = part
    lax.fori_loop(FACE // 4, FACE - 1, ship, 0)
    for axis in range(3):
        parcel(axis, FACE - 1).start()
    for k in range(1, n_grp):
        gram_third(k).start()
    for axis in range(3):
        pack_into(recvs[axis], face_index(axis), axis, me)

    def link(p, state):
        seen, order, last, before = state
        owner = wanted_tiles[p] // held
        hit = lane == owner
        turn = jnp.sum(jnp.where(hit, seen, 0), axis=1, keepdims=True)
        order = jnp.where(lane == p, owner * 2 + jnp.minimum(turn, 1), order)
        seen = jnp.where(hit, 1, seen)
        mine = lane == user_tiles[p]
        earlier = jnp.sum(jnp.where(mine, last, 0), axis=1, keepdims=True)
        before = jnp.where(lane == p, earlier, before)
        last = jnp.where(mine, p + 1, last)
        return seen, order, last, before

    _, order, last, before = lax.fori_loop(0, pairs, link, (zero,) * 4)
    row = lax.broadcasted_iota(jnp.int32, (8, 128), 0)
    table[...] = jnp.where(
        row == 0, order, jnp.where(row == 1, before, jnp.where(row == 2, last, 0))
    )
    table_copy = pltpu.make_async_copy(table, table_s, local_sems.at[2])
    table_copy.start()
    count_copy.wait()

    def weigh(p, carry):
        weights[p] = (counted[p].astype(jnp.float32) * ALPHA).astype(jnp.bfloat16)
        return carry

    lax.fori_loop(0, pairs, weigh, 0)
    chain[0] = jnp.zeros((tile, rank), jnp.float32)
    table_copy.wait()

    gather_end()
    for k in range(1, n_grp):
        gram_third(k).wait()

    def wait_parcel(step, carry):
        for axis in range(3):
            parcel(axis, step).wait()
        return carry

    lax.fori_loop(1, FACE, wait_parcel, 0)

    def take(p, carry):
        slot = table_s[0, p]
        owner, turn = slot // 2, slot % 2
        ob, og = owner // n_grp, owner % n_grp
        at, of = (og // SIDE, og % SIDE, ob // 2), ob % 2
        for axis, (start, rows) in enumerate(SHARE):
            face = (at[(axis + 1) % 3] * SIDE + at[(axis + 2) % 3]) * 2 + of
            tiles[p, start:start + rows] = recvs[axis][face, at[axis], turn]
        return carry

    lax.fori_loop(0, pairs, take, 0)

    def accumulate(with_rhs):
        group = 4

        def several(i, carry):
            backs = []
            for j in range(group):
                p = i * group + j
                factors = tiles[p]
                weight = weights[p].astype(jnp.float32)
                scores = lax.dot_general(
                    low[tile_place(user_tiles[p])], factors, (((1,), (1,)), ((), ())),
                    preferred_element_type=jnp.float32,
                )
                scaled = (weight * scores).astype(jnp.bfloat16)
                back = jnp.dot(scaled, factors, preferred_element_type=jnp.float32)
                if with_rhs:
                    confidence = jnp.where(weight > 0, 1.0 + weight, 0.0).astype(jnp.bfloat16)
                    back = jnp.dot(
                        confidence, factors, preferred_element_type=jnp.float32
                    ) - back
                backs.append(back)
            for j in range(group):
                p = i * group + j
                chain[p + 1] = chain[table_s[1, p]] + backs[j]
            return carry

        lax.fori_loop(0, pairs // group, several, 0)

    near, far = (y, x), (x, y)

    def partial(t, away, end):
        u = 2 * (end * SIDE + away) if t == 0 else 2 * (away * SIDE + end) + 1
        return chain[table_s[2, u]]

    def sum_first(t, k, m):
        to = mesh_id(moved(place, 1 - t, k), core)
        return [
            remote(
                src.at[t, k, m], dst.at[t, k, m], first_sems.at[0, i, t, k, m],
                first_sems.at[1, i, t, k, m], to,
            )
            for i, (src, dst) in enumerate(((part_u, first_u), (part_q, first_q)))
        ]

    def sum_second(t, m):
        to = mesh_id(moved(place, t, m), core)
        return [
            remote(
                src.at[t, m], dst.at[t, m], second_sems.at[0, i, t, m],
                second_sems.at[1, i, t, m], to,
            )
            for i, (src, dst) in enumerate(((sum_u, second_u), (sum_q, second_q)))
        ]

    turns = tuple(range(1, SIDE)) + (0,)

    def reduce_start():
        for m in turns:
            for k in range(1, SIDE):
                for t in range(2):
                    whole, unit = quantize(
                        partial(t, (near[t] + k) % SIDE, (far[t] + m) % SIDE)
                    )
                    part_q[t, k, m] = whole
                    part_u[t, k, m] = unit
                    for copy in sum_first(t, k, m):
                        copy.start()

    def reduce_finish():
        for m in turns:
            for t in range(2):
                total = partial(t, near[t], (far[t] + m) % SIDE)
                for k in range(1, SIDE):
                    for copy in sum_first(t, k, m):
                        copy.wait()
                    total = total + restore(first_q[t, k, m], first_u[t, k, m])
                if m == 0:
                    sums[t] = total
                else:
                    whole, unit = quantize(total)
                    sum_q[t, m] = whole
                    sum_u[t, m] = unit
                    for copy in sum_second(t, m):
                        copy.start()
        totals = []
        for t in range(2):
            total = sums[t]
            for m in range(1, SIDE):
                for copy in sum_second(t, m):
                    copy.wait()
                total = total + restore(second_q[t, m], second_u[t, m])
            totals.append(total)
        return jnp.concatenate(totals, axis=0)

    def gram_term(vectors):
        return (
            jnp.dot(vectors, gram_c[...].reshape(rank, rank), precision=lax.Precision.HIGHEST,
                    preferred_element_type=jnp.float32)
            + REG * vectors
        )

    def row_sum(left, right):
        return jnp.sum(left * right, axis=1, keepdims=True)

    accumulate(True)
    reduce_start()
    local[...] = gram_term(prior[...])
    start = reduce_finish() - local[...]
    residual[...] = start
    direction[...] = start
    out[...] = prior[...]

    def iterate(step, norm_now):
        d_low = direction[...].astype(jnp.bfloat16)
        low[y * SIDE + x] = d_low[:tile]
        low[PLANE + x * SIDE + y] = d_low[tile:]
        gather_begin()
        local[...] = gram_term(direction[...])
        gather_onward()
        gather_end()
        accumulate(False)
        reduce_start()
        image = local[...] + reduce_finish()
        d = direction[...]
        alpha = norm_now / (row_sum(d, image) + EPS)
        out[...] = out[...] + alpha * d
        r = residual[...] - alpha * image
        residual[...] = r
        fresh = row_sum(r, r)
        direction[...] = r + fresh / (norm_now + EPS) * d
        return fresh

    lax.fori_loop(0, ITERS, iterate, row_sum(start, start))


def body(user_prior, item_factors, user_tiles, item_tiles, counts):
    n_blk = lax.axis_size("blk")
    n_grp = lax.axis_size("grp")
    n_all = n_blk * n_grp
    pairs, tile, _ = counts.shape
    rank = item_factors.shape[1]
    users = 2 * n_grp
    own = user_prior.shape[0]
    held = item_factors.shape[0] // tile
    grows = rank // n_grp
    vmem = pl.BlockSpec(memory_space=pltpu.VMEM)
    smem = pl.BlockSpec(memory_space=pltpu.SMEM)
    dma = pltpu.SemaphoreType.DMA
    low_type, whole_type, full = jnp.bfloat16, jnp.int16, jnp.float32
    return pl.pallas_call(
        functools.partial(kernel, n_blk, n_grp),
        out_shape=jax.ShapeDtypeStruct((own, rank), full),
        in_specs=[smem, smem, vmem, vmem, pl.BlockSpec(memory_space=pl.ANY)],
        out_specs=vmem,
        scratch_shapes=[
            pltpu.VMEM((1, 128), jnp.int32),
            pltpu.VMEM((n_all, 1, 128), jnp.int32),
            pltpu.SMEM((n_all, 1, 128), jnp.int32),
            pltpu.VMEM((8, 128), jnp.int32),
            pltpu.SMEM((8, 128), jnp.int32),
            *(pltpu.VMEM((SIDE, held, rows, rank), low_type) for _, rows in SHARE),
            *(pltpu.VMEM((FACE, SIDE, 2, rows, rank), low_type) for _, rows in SHARE),
            *(pltpu.VMEM((FACE, SIDE, 2, rows, rank), low_type) for _, rows in SHARE),
            pltpu.VMEM((pairs, tile, rank), low_type),
            pltpu.VMEM((pairs, tile, tile), jnp.int32),
            pltpu.VMEM((pairs, tile, tile), low_type),
            pltpu.VMEM((users, tile, rank), low_type),
            pltpu.VMEM((pairs + 1, tile, rank), full),
            pltpu.VMEM((n_grp, grows, rank), full),
            pltpu.VMEM((n_grp, grows, rank), full),
            pltpu.VMEM((n_blk, grows, rank), full),
            pltpu.VMEM((n_grp, grows, rank), full),
            pltpu.VMEM((2, grows, rank), full),
            pltpu.VMEM((2, SIDE, SIDE, tile, rank), whole_type),
            pltpu.VMEM((2, SIDE, SIDE, 1, rank), full),
            pltpu.VMEM((2, SIDE, SIDE, tile, rank), whole_type),
            pltpu.VMEM((2, SIDE, SIDE, 1, rank), full),
            pltpu.VMEM((2, SIDE, tile, rank), whole_type),
            pltpu.VMEM((2, SIDE, 1, rank), full),
            pltpu.VMEM((2, SIDE, tile, rank), whole_type),
            pltpu.VMEM((2, SIDE, 1, rank), full),
            pltpu.VMEM((2, tile, rank), full),
            pltpu.VMEM((own, rank), full),
            pltpu.VMEM((own, rank), full),
            pltpu.VMEM((own, rank), full),
            dma((2, n_all)),
            dma((2, 3, 4)),
            dma((2, 3, FACE)),
            dma((2, 2, SIDE)),
            dma((2, 2, SIDE, SIDE)),
            dma((2, 2, 2, SIDE, SIDE)),
            dma((2, 2, 2, SIDE)),
            dma((3, 2, n_grp)),
            dma((3,)),
        ],
        compiler_params=pltpu.CompilerParams(
            collective_id=0, has_side_effects=True, vmem_limit_bytes=60 << 20
        ),
        name="als",
    )(item_tiles, user_tiles, item_factors.reshape(held, tile, rank), user_prior, counts)


def solution(mesh):
    in_specs = (
        P(("blk", "grp"), None),
        P(("blk", "grp"), None),
        P(("blk", "grp")),
        P(("blk", "grp")),
        P(("blk", "grp"), None, None),
    )
    out_specs = P(("blk", "grp"), None)
    return jax.shard_map(body, mesh=mesh, in_specs=in_specs, out_specs=out_specs, check_vma=False)
```

time: 794 us -> 251 us (0.32)
  waiting for transfers between devices: 575 us -> 0 us
  Pallas kernels: 0 us -> 245 us
  local copies, waits for them, and re-layouts: 78.8 us -> 1.57 us
  matrix products: 69 us -> 0 us
  blocking collectives: 20.5 us -> 0 us
  other arithmetic: 19.5 us -> 0 us
  between operations: 16 us -> 0.01 us
    psum x5 -> x0, waiting for transfers between devices: 470 us -> none  [the longest x3 306 us: body(): image = gram_term(direction) + lax.psum(pair_part, 'grp')]
    pallas_call x0 -> x1, Pallas kernels: none -> 245 us  [body(): pl.pallas_call(functools.partial(kernel, n_blk, n_grp), out_shape=jax.Sha...]
    all_gather x1 -> x0, waiting for transfers between devices: 105 us -> none  [body(): whole = lax.all_gather(user_prior, 'grp', axis=0, tiled=True)]
    dot_general x15 -> x0, matrix products: 69 us -> none  [the longest x4 23.8 us: one_round(): jnp.einsum('tb,bur->tur', selector, back, precision=lax.Precision.HIGHEST)]
    unnamed x32 -> x1, local copies, waits for them, and re-layouts: 28.6 us -> 1.57 us
    gather x6 -> x0, local copies, waits for them, and re-layouts: 20.6 us -> none  [the longest x1 8.34 us: fetch_tiles(): picked = jnp.take(held, jnp.maximum(wanted, 0), axis=0)]
    all_to_all x1 -> x0, blocking collectives: 20.5 us -> none  [fetch_tiles(): lax.all_to_all(requests, ('blk', 'grp'), split_axis=0, concat_axis=0, til...]
    while x7 -> x0, local copies, waits for them, and re-layouts: 16.5 us -> none  [the longest x5 16.5 us: accumulate(): totals = lax.fori_loop(0, rounds, one_round, start_state)]
  transfers between devices with their start and end apart: 7 -> 0, of which waited for: 6 -> 0; matrix products, arithmetic and copies ran while one was open for 6% -> 0% of each run, Pallas kernels for 0% -> 0%
where the time goes in v2:
time: 251 us; the launch traced here: 247 us
  Pallas kernels  245 us (98%)
    pallas_call x1, Pallas kernels, body(): pl.pallas_call(functools.partial(kernel, n_blk, n_grp), out_shape=jax.Sha...  245 us

profile of v2, /device:TPU:0, one launch (start us, length us, event | category | flops | bytes accessed | tf_op | source)
XLA Modules:
  0.0 247.0 jit_solution(11770137454540393116)
XLA Ops:
  0.0 245.4 %als.1 = f32[256,128]{1,0:T(8,128)} custom-call(s32[64]{0:T(128)} %wanted_tiles.1, s32[64]{0:T(128)} %user_tiles.1, bf16[32,128,128]{2,1,0:T(8,128)(2,1)} %bitcast.1, f32[256,128]{1,0:T(8,128)} %prior.1, s32[64,128,128]{2,1,0:T(8,128)} %counts.1), custom_call_target="tpu_custom_call" | custom-call | tf_op jit(solution)/shard_map/als/pallas_call | solution.py:518
  245.4 1.6 copy.7

commit v3 on v2

--- a/solution.py
+++ b/solution.py
@@ -16,6 +16,9 @@
 FACE = 2 * PLANE
 LEVELS = 32700.0
 SHARE = ((0, 48), (48, 48), (96, 32))
+AROUND = (0, 1, 3, 2)
+CLOSE = 3
+SHIFTS = (1, 3, 4, 12, 2, 8, 5, 7, 13, 15, 6, 9, 11, 14, 10)
 MESH = pl.DeviceIdType.MESH
 
 
@@ -71,8 +74,8 @@
     wanted_tiles, user_tiles, items, prior, counts,
     out,
     req, reqs, want, table, table_s,
-    ring0, ring1, ring2, send0, send1, send2, recv0, recv1, recv2,
-    tiles, counted, weights, low, chain,
+    ring0, ring1, ring2, far0, far1, far2, send0, send1, send2, recv0, recv1, recv2,
+    tiles, counted, weights, pulls, scaled, low, chain,
     gram_own, gram_a, gram_b, gram_c, gram_t,
     part_q, part_u, first_q, first_u, sum_q, sum_u, second_q, second_u, sums,
     residual, direction, local,
@@ -86,6 +89,7 @@
     me = b * n_grp + g
     pairs, tile, rank = tiles.shape
     held = items.shape[0]
+    fars = (far0, far1, far2)
     rings, sends, recvs = (ring0, ring1, ring2), (send0, send1, send2), (recv0, recv1, recv2)
 
     count_copy = pltpu.make_async_copy(counts, counted, local_sems.at[0])
@@ -124,7 +128,7 @@
 
     def keep(i, carry):
         for axis, (start, rows) in enumerate(SHARE):
-            rings[axis][place[axis], i] = items[i, start:start + rows]
+            rings[axis][0, i] = items[i, start:start + rows]
         return carry
 
     lax.fori_loop(0, held, keep, 0)
@@ -144,14 +148,12 @@
 
     def ring_copy(axis, kind):
         start, rows = SHARE[axis]
-        ring = rings[axis]
-        here = place[axis]
+        source = 2 if kind % 2 == 0 else 1
         if kind < 2:
-            src, dst = items.at[:, pl.ds(start, rows)], ring.at[here]
+            src, dst = items.at[:, pl.ds(start, rows)], rings[axis].at[source]
         else:
-            origin = (here + SIDE - 1) % SIDE if kind == 2 else (here + 1) % SIDE
             half = pl.ds(0 if kind == 2 else held // 2, held // 2)
-            src = dst = ring.at[origin, half]
+            src, dst = rings[axis].at[source, half], fars[axis].at[half]
         to = moved(place, axis, 1 if kind % 2 == 0 else SIDE - 1)
         return remote(
             src, dst, ring_sems.at[0, axis, kind], ring_sems.at[1, axis, kind],
@@ -260,9 +262,13 @@
     want_copy.wait()
     for k in range(1, n_blk):
         gram_second(k).start()
-    for axis in range(3):
-        for kind in range(2, 4):
-            ring_copy(axis, kind).wait()
+
+    def face_shift(turn):
+        words = [sum(v << 4 * j for j, v in enumerate(SHIFTS[i:i + 7])) for i in (0, 7, 14)]
+        i = turn // 2
+        word = jnp.where(i < 7, words[0], jnp.where(i < 14, words[1], words[2]))
+        shift = lax.shift_right_logical(jnp.int32(word), 4 * (i % 7)) % 16
+        return shift * 2 + turn % 2
 
     def face_target(axis, step):
         a, c = step // 2 // SIDE, step // 2 % SIDE
@@ -272,32 +278,44 @@
     def face_index(axis):
         return (place[(axis + 1) % 3] * SIDE + place[(axis + 2) % 3]) * 2 + core
 
-    def pack_into(ref, slot, axis, to):
-        for w in range(SIDE):
+    def pack_into(ref, slot, axis, to, which):
+        for i in which:
+            w = (place[axis] + AROUND[i]) % SIDE
             pair = want[to, 0, flat_id(put_at(place, axis, w), core)]
-            ref[slot, w, 0] = rings[axis][w, pair % 256]
-            ref[slot, w, 1] = rings[axis][w, pair // 256]
-
-    def pack(step):
+            for j, held_at in enumerate((pair % 256, pair // 256)):
+                ref[slot, i, j] = rings[axis][i, held_at] if i < CLOSE else fars[axis][held_at]
+
+    levels = (tuple(range(CLOSE)), tuple(range(CLOSE, SIDE)))
+
+    def pack(level, step):
         for axis in range(3):
             to, to_core = face_target(axis, step)
-            pack_into(sends[axis], step, axis, flat_id(to, to_core))
-
-    def parcel(axis, step):
+            pack_into(sends[axis], step, axis, flat_id(to, to_core), levels[level])
+
+    def parcel(level, axis, step):
         to, to_core = face_target(axis, step)
-        return remote(
-            sends[axis].at[step], recvs[axis].at[face_index(axis)],
-            tile_sems.at[0, axis, step], tile_sems.at[1, axis, step], mesh_id(to, to_core),
-        )
-
-    def ship(step, carry):
-        pack(step + 1)
+        part = pl.ds(levels[level][0], len(levels[level]))
+        return remote(
+            sends[axis].at[step, part], recvs[axis].at[face_index(axis), part],
+            tile_sems.at[0, level, axis, step], tile_sems.at[1, level, axis, step],
+            mesh_id(to, to_core),
+        )
+
+    def ship(level, first, last):
+        pack(level, face_shift(first))
+
+        def one(turn, carry):
+            pack(level, face_shift(turn + 1))
+            for axis in range(3):
+                parcel(level, axis, face_shift(turn)).start()
+            return carry
+
+        lax.fori_loop(first, last - 1, one, 0)
         for axis in range(3):
-            parcel(axis, step).start()
-        return carry
-
-    pack(1)
-    lax.fori_loop(1, FACE // 4, ship, 0)
+            parcel(level, axis, face_shift(last - 1)).start()
+
+    turns_all = 2 * len(SHIFTS)
+    ship(0, 0, 8)
     for k in range(1, n_blk):
         gram_second(k).wait()
     part = gram_t[0]
@@ -305,13 +323,20 @@
         part = part + gram_b[k]
     gram_t[1] = part
     gram_c[g] = part
-    lax.fori_loop(FACE // 4, FACE - 1, ship, 0)
+    ship(0, 8, turns_all)
     for axis in range(3):
-        parcel(axis, FACE - 1).start()
+        for kind in range(2, 4):
+            ring_copy(axis, kind).wait()
+    pack(0, 1)
+    pack(1, 1)
+    ship(1, 0, turns_all)
+    for level in range(2):
+        for axis in range(3):
+            parcel(level, axis, 1).start()
     for k in range(1, n_grp):
         gram_third(k).start()
     for axis in range(3):
-        pack_into(recvs[axis], face_index(axis), axis, me)
+        pack_into(recvs[axis], face_index(axis), axis, me, range(SIDE))
 
     def link(p, state):
         seen, order, last, before = state
@@ -336,7 +361,9 @@
     count_copy.wait()
 
     def weigh(p, carry):
-        weights[p] = (counted[p].astype(jnp.float32) * ALPHA).astype(jnp.bfloat16)
+        weight = counted[p].astype(jnp.float32) * ALPHA
+        weights[p] = weight.astype(jnp.bfloat16)
+        pulls[p] = jnp.where(weight > 0, 1.0 + weight, 0.0).astype(jnp.bfloat16)
         return carry
 
     lax.fori_loop(0, pairs, weigh, 0)
@@ -348,51 +375,59 @@
         gram_third(k).wait()
 
     def wait_parcel(step, carry):
-        for axis in range(3):
-            parcel(axis, step).wait()
+        for level in range(2):
+            for axis in range(3):
+                parcel(level, axis, step).wait()
         return carry
 
     lax.fori_loop(1, FACE, wait_parcel, 0)
 
-    def take(p, carry):
-        slot = table_s[0, p]
-        owner, turn = slot // 2, slot % 2
-        ob, og = owner // n_grp, owner % n_grp
-        at, of = (og // SIDE, og % SIDE, ob // 2), ob % 2
-        for axis, (start, rows) in enumerate(SHARE):
-            face = (at[(axis + 1) % 3] * SIDE + at[(axis + 2) % 3]) * 2 + of
-            tiles[p, start:start + rows] = recvs[axis][face, at[axis], turn]
+    def take(i, carry):
+        for j in range(4):
+            p = i * 4 + j
+            slot = table_s[0, p]
+            owner, turn = slot // 2, slot % 2
+            ob, og = owner // n_grp, owner % n_grp
+            at, of = (og // SIDE, og % SIDE, ob // 2), ob % 2
+            for axis, (start, rows) in enumerate(SHARE):
+                face = (at[(axis + 1) % 3] * SIDE + at[(axis + 2) % 3]) * 2 + of
+                ahead = (at[axis] + SIDE - place[axis]) % SIDE
+                ahead = jnp.where(ahead >= 2, 5 - ahead, ahead)
+                tiles[p, start:start + rows] = recvs[axis][face, ahead, turn]
         return carry
 
-    lax.fori_loop(0, pairs, take, 0)
+    lax.fori_loop(0, pairs // 4, take, 0)
+
+    group = 8
 
     def accumulate(with_rhs):
-        group = 4
-
-        def several(i, carry):
+        def score(i, carry):
+            for j in range(group):
+                p = i * group + j
+                scores = lax.dot_general(
+                    low[tile_place(user_tiles[p])], tiles[p], (((1,), (1,)), ((), ())),
+                    preferred_element_type=jnp.float32,
+                )
+                scaled[p] = (weights[p].astype(jnp.float32) * scores).astype(jnp.bfloat16)
+            return carry
+
+        lax.fori_loop(0, pairs // group, score, 0)
+
+        def spread(i, carry):
             backs = []
             for j in range(group):
                 p = i * group + j
-                factors = tiles[p]
-                weight = weights[p].astype(jnp.float32)
-                scores = lax.dot_general(
-                    low[tile_place(user_tiles[p])], factors, (((1,), (1,)), ((), ())),
-                    preferred_element_type=jnp.float32,
-                )
-                scaled = (weight * scores).astype(jnp.bfloat16)
-                back = jnp.dot(scaled, factors, preferred_element_type=jnp.float32)
+                back = jnp.dot(scaled[p], tiles[p], preferred_element_type=jnp.float32)
                 if with_rhs:
-                    confidence = jnp.where(weight > 0, 1.0 + weight, 0.0).astype(jnp.bfloat16)
-                    back = jnp.dot(
-                        confidence, factors, preferred_element_type=jnp.float32
-                    ) - back
+                    pulled = jnp.dot(pulls[p], tiles[p], preferred_element_type=jnp.float32)
+                    back = pulled - back
                 backs.append(back)
             for j in range(group):
                 p = i * group + j
                 chain[p + 1] = chain[table_s[1, p]] + backs[j]
             return carry
 
-        lax.fori_loop(0, pairs // group, several, 0)
+        lax.fori_loop(0, pairs // group, spread, 0)
 
     near, far = (y, x), (x, y)
 
@@ -526,11 +561,14 @@
             pltpu.SMEM((n_all, 1, 128), jnp.int32),
             pltpu.VMEM((8, 128), jnp.int32),
             pltpu.SMEM((8, 128), jnp.int32),
-            *(pltpu.VMEM((SIDE, held, rows, rank), low_type) for _, rows in SHARE),
+            *(pltpu.VMEM((CLOSE, held, rows, rank), low_type) for _, rows in SHARE),
+            *(pltpu.VMEM((held, rows, rank), low_type) for _, rows in SHARE),
             *(pltpu.VMEM((FACE, SIDE, 2, rows, rank), low_type) for _, rows in SHARE),
             *(pltpu.VMEM((FACE, SIDE, 2, rows, rank), low_type) for _, rows in SHARE),
             pltpu.VMEM((pairs, tile, rank), low_type),
             pltpu.VMEM((pairs, tile, tile), jnp.int32),
+            pltpu.VMEM((pairs, tile, tile), low_type),
+            pltpu.VMEM((pairs, tile, tile), low_type),
             pltpu.VMEM((pairs, tile, tile), low_type),
             pltpu.VMEM((users, tile, rank), low_type),
             pltpu.VMEM((pairs + 1, tile, rank), full),
@@ -553,7 +591,7 @@
             pltpu.VMEM((own, rank), full),
             dma((2, n_all)),
             dma((2, 3, 4)),
-            dma((2, 3, FACE)),
+            dma((2, 2, 3, FACE)),
             dma((2, 2, SIDE)),
             dma((2, 2, SIDE, SIDE)),
             dma((2, 2, 2, SIDE, SIDE)),

time: 251 us -> 232 us (0.924)
  the two profiles are of different devices: /device:TPU:0 before, /device:TPU:32 now
where the time goes in v3:
time: 232 us; the launch traced here: 231 us
  Pallas kernels  230 us (99%)
    pallas_call x1, Pallas kernels, body(): pl.pallas_call(functools.partial(kernel, n_blk, n_grp), out_shape=jax.Sha...  230 us

profile of v3, /device:TPU:32, one launch (start us, length us, event | category | flops | bytes accessed | tf_op | source)
XLA Modules:
  0.0 231.5 jit_solution(2473794979325315316)
XLA Ops:
  0.0 229.9 %als.1 = f32[256,128]{1,0:T(8,128)} custom-call(s32[64]{0:T(128)} %wanted_tiles.1, s32[64]{0:T(128)} %user_tiles.1, bf16[32,128,128]{2,1,0:T(8,128)(2,1)} %bitcast.1, f32[256,128]{1,0:T(8,128)} %prior.1, s32[64,128,128]{2,1,0:T(8,128)} %counts.1), custom_call_target="tpu_custom_call" | custom-call | tf_op jit(solution)/shard_map/als/pallas_call | solution.py:553
  229.9 1.6 copy.7

commit v4 on v3

--- a/solution.py
+++ b/solution.py
@@ -14,11 +14,12 @@
 SIDE = 4
 PLANE = SIDE * SIDE
 FACE = 2 * PLANE
+PEERS = 73
 LEVELS = 32700.0
 SHARE = ((0, 48), (48, 48), (96, 32))
 AROUND = (0, 1, 3, 2)
 CLOSE = 3
-SHIFTS = (1, 3, 4, 12, 2, 8, 5, 7, 13, 15, 6, 9, 11, 14, 10)
+SHIFTS = (1, 3, 4, 12, 2, 8, 5, 15, 7, 13, 6, 14, 9, 11, 10)
 MESH = pl.DeviceIdType.MESH
 
 
@@ -75,7 +76,7 @@
     out,
     req, reqs, want, table, table_s,
     ring0, ring1, ring2, far0, far1, far2, send0, send1, send2, recv0, recv1, recv2,
-    tiles, counted, weights, pulls, scaled, low, chain,
+    tiles, counted, weights, pulls, scaled, low0, low1, chain,
     gram_own, gram_a, gram_b, gram_c, gram_t,
     part_q, part_u, first_q, first_u, sum_q, sum_u, second_q, second_u, sums,
     residual, direction, local,
@@ -89,23 +90,47 @@
     me = b * n_grp + g
     pairs, tile, rank = tiles.shape
     held = items.shape[0]
+    half = tile // 2
     fars = (far0, far1, far2)
+    lows = (low0, low1)
     rings, sends, recvs = (ring0, ring1, ring2), (send0, send1, send2), (recv0, recv1, recv2)
+
+    def half_rows(ref, h):
+        return jnp.concatenate(
+            [ref[t * tile + h * half:t * tile + (h + 1) * half] for t in range(2)], axis=0
+        )
+
+    def lower(h, vectors):
+        d_low = vectors.astype(jnp.bfloat16)
+        lows[h][y * SIDE + x] = d_low[:half]
+        lows[h][PLANE + x * SIDE + y] = d_low[half:]
 
     count_copy = pltpu.make_async_copy(counts, counted, local_sems.at[0])
     count_copy.start()
 
-    def other(step):
-        b_to = (b + step // n_grp) % n_blk
-        return b_to, (g + step % n_grp) % n_grp
+    def same_x(i):
+        return (place[0], (y + i // 8) % SIDE, (z + i // 2) % SIDE), (core + i) % 2
+
+    def same_y(i):
+        return ((x + 1 + i // 8) % SIDE, place[1], (z + i // 2) % SIDE), (core + i) % 2
+
+    def same_z(i):
+        return ((x + 1 + i // 2 % 3) % SIDE, (y + 1 + i // 6) % SIDE, place[2]), (core + i) % 2
+
+    families = ((same_x, 1, 32, 0), (same_y, 0, 24, 32), (same_z, 0, 18, 56))
+
+    def for_peers(act):
+        for family, first, last, base in families:
+            def one(i, carry):
+                act(mesh_id(*family(i)), base + i)
+                return carry
+
+            lax.fori_loop(first, last, one, 0)
 
     barrier = pltpu.get_barrier_semaphore()
-
-    def greet(step, carry):
-        pl.semaphore_signal(barrier, inc=1, device_id=other(step), device_id_type=MESH)
-        return carry
-
-    lax.fori_loop(1, n_all, greet, 0)
+    for_peers(
+        lambda to, i: pl.semaphore_signal(barrier, inc=1, device_id=to, device_id_type=MESH)
+    )
 
     lane = lax.broadcasted_iota(jnp.int32, (1, 128), 1)
     zero = jnp.zeros((1, 128), jnp.int32)
@@ -123,8 +148,8 @@
     asked = first + 256 * second
     req[...] = asked
     reqs[me] = asked
-    low[y * SIDE + x] = prior[:tile].astype(jnp.bfloat16)
-    low[PLANE + x * SIDE + y] = prior[tile:].astype(jnp.bfloat16)
+    for h in range(2):
+        lower(h, half_rows(prior, h))
 
     def keep(i, carry):
         for axis, (start, rows) in enumerate(SHARE):
@@ -133,18 +158,12 @@
 
     lax.fori_loop(0, held, keep, 0)
 
-    pl.semaphore_wait(barrier, n_all - 1)
-
-    def request(step):
-        return remote(
-            req, reqs.at[me], req_sems.at[0, step], req_sems.at[1, step], other(step)
-        )
-
-    def send_request(step, carry):
-        request(step).start()
-        return carry
-
-    lax.fori_loop(1, n_all, send_request, 0)
+    pl.semaphore_wait(barrier, PEERS)
+
+    def request(to, i):
+        return remote(req, reqs.at[me], req_sems.at[0, i], req_sems.at[1, i], to)
+
+    for_peers(lambda to, i: request(to, i).start())
 
     def ring_copy(axis, kind):
         start, rows = SHARE[axis]
@@ -169,42 +188,43 @@
             return y * SIDE + (x + SIDE - m) % SIDE
         return PLANE + x * SIDE + (y + SIDE - m) % SIDE
 
-    def gather_a(t, k):
-        ref = low.at[low_place(t, 0)]
+    def gather_a(h, t, k):
+        ref = lows[h].at[low_place(t, 0)]
         return remote(
-            ref, ref, gather_one.at[0, t, k], gather_one.at[1, t, k],
+            ref, ref, gather_one.at[0, h, t, k], gather_one.at[1, h, t, k],
             mesh_id(moved(place, t, k), core),
         )
 
-    def gather_b(t, k, m):
-        ref = low.at[low_place(t, m)]
+    def gather_b(h, t, k, m):
+        ref = lows[h].at[low_place(t, m)]
         return remote(
-            ref, ref, gather_two.at[0, t, k, m], gather_two.at[1, t, k, m],
+            ref, ref, gather_two.at[0, h, t, k, m], gather_two.at[1, h, t, k, m],
             mesh_id(moved(place, 1 - t, k), core),
         )
 
-    def gather_begin():
+    def gather_begin(h):
         for k in range(1, SIDE):
             for t in range(2):
-                gather_a(t, k).start()
+                gather_a(h, t, k).start()
         for k in range(1, SIDE):
             for t in range(2):
-                gather_b(t, k, 0).start()
-
-    def gather_onward():
+                gather_b(h, t, k, 0).start()
+
+    def gather_onward(h):
         for m in range(1, SIDE):
             for t in range(2):
-                gather_a(t, m).wait()
+                gather_a(h, t, m).wait()
                 for k in range(1, SIDE):
-                    gather_b(t, k, m).start()
-
-    def gather_end():
+                    gather_b(h, t, k, m).start()
+
+    def gather_end(h):
         for m in range(SIDE):
             for k in range(1, SIDE):
                 for t in range(2):
-                    gather_b(t, k, m).wait()
-
-    gather_begin()
+                    gather_b(h, t, k, m).wait()
+
+    gather_begin(0)
+    gather_begin(1)
 
     chunk = min(8, held)
 
@@ -239,39 +259,28 @@
     for k in range(1, n_grp):
         gram_first(k).start()
 
+    for_peers(lambda to, i: request(to, i).wait())
+    want_copy = pltpu.make_async_copy(reqs, want, local_sems.at[1])
+    want_copy.start()
     for axis in range(3):
         for kind in range(2):
             ring_copy(axis, kind).wait()
             ring_copy(axis, kind + 2).start()
-
-    gather_onward()
-
-    def wait_request(step, carry):
-        request(step).wait()
-        return carry
-
-    lax.fori_loop(1, n_all, wait_request, 0)
-    want_copy = pltpu.make_async_copy(reqs, want, local_sems.at[1])
-    want_copy.start()
-    for k in range(1, n_grp):
-        gram_first(k).wait()
-    part = gram_own[g]
-    for k in range(1, n_grp):
-        part = part + gram_a[k]
-    gram_t[0] = part
     want_copy.wait()
-    for k in range(1, n_blk):
-        gram_second(k).start()
 
     def face_shift(turn):
         words = [sum(v << 4 * j for j, v in enumerate(SHIFTS[i:i + 7])) for i in (0, 7, 14)]
-        i = turn // 2
+        last = turn >= 28
+        i = jnp.where(last, 14, turn // 4 * 2 + turn % 2)
+        flip = jnp.where(last, turn % 2, turn // 2 % 2)
         word = jnp.where(i < 7, words[0], jnp.where(i < 14, words[1], words[2]))
         shift = lax.shift_right_logical(jnp.int32(word), 4 * (i % 7)) % 16
-        return shift * 2 + turn % 2
+        return shift * 2 + flip
 
     def face_target(axis, step):
         a, c = step // 2 // SIDE, step // 2 % SIDE
+        a = jnp.where(core == 0, a, (SIDE - a) % SIDE)
+        c = jnp.where(core == 0, c, (SIDE - c) % SIDE)
         to = moved(moved(place, (axis + 1) % 3, a), (axis + 2) % 3, c)
         return to, (core + step) % 2
 
@@ -315,7 +324,19 @@
             parcel(level, axis, face_shift(last - 1)).start()
 
     turns_all = 2 * len(SHIFTS)
-    ship(0, 0, 8)
+    ship(0, 0, 4)
+    gather_onward(0)
+    gather_onward(1)
+    for k in range(1, n_grp):
+        gram_first(k).wait()
+    part = gram_own[g]
+    for k in range(1, n_grp):
+        part = part + gram_a[k]
+    gram_t[0] = part
+    ship(0, 4, 16)
+    for k in range(1, n_blk):
+        gram_second(k).start()
+    ship(0, 16, turns_all)
     for k in range(1, n_blk):
         gram_second(k).wait()
     part = gram_t[0]
@@ -323,7 +344,6 @@
         part = part + gram_b[k]
     gram_t[1] = part
     gram_c[g] = part
-    ship(0, 8, turns_all)
     for axis in range(3):
         for kind in range(2, 4):
             ring_copy(axis, kind).wait()
@@ -367,10 +387,12 @@
         return carry
 
     lax.fori_loop(0, pairs, weigh, 0)
-    chain[0] = jnp.zeros((tile, rank), jnp.float32)
+    for h in range(2):
+        chain[h, 0] = jnp.zeros((half, rank), jnp.float32)
     table_copy.wait()
 
-    gather_end()
+    gather_end(0)
+    gather_end(1)
     for k in range(1, n_grp):
         gram_third(k).wait()
 
@@ -400,15 +422,17 @@
 
     group = 8
 
-    def accumulate(with_rhs):
+    def accumulate(h, with_rhs):
+        part = slice(h * half, (h + 1) * half)
+
         def score(i, carry):
             for j in range(group):
                 p = i * group + j
                 scores = lax.dot_general(
-                    low[tile_place(user_tiles[p])], tiles[p], (((1,), (1,)), ((), ())),
+                    lows[h][tile_place(user_tiles[p])], tiles[p], (((1,), (1,)), ((), ())),
                     preferred_element_type=jnp.float32,
                 )
-                scaled[p] = (weights[p].astype(jnp.float32) * scores).astype(jnp.bfloat16)
+                scaled[p] = (weights[p, part].astype(jnp.float32) * scores).astype(jnp.bfloat16)
             return carry
 
         lax.fori_loop(0, pairs // group, score, 0)
@@ -419,79 +443,83 @@
                 p = i * group + j
                 back = jnp.dot(scaled[p], tiles[p], preferred_element_type=jnp.float32)
                 if with_rhs:
-                    pulled = jnp.dot(pulls[p], tiles[p], preferred_element_type=jnp.float32)
+                    pulled = jnp.dot(
+                        pulls[p, part], tiles[p], preferred_element_type=jnp.float32
+                    )
                     back = pulled - back
                 backs.append(back)
             for j in range(group):
                 p = i * group + j
-                chain[p + 1] = chain[table_s[1, p]] + backs[j]
+                chain[h, p + 1] = chain[h, table_s[1, p]] + backs[j]
             return carry
 
         lax.fori_loop(0, pairs // group, spread, 0)
 
     near, far = (y, x), (x, y)
 
-    def partial(t, away, end):
+    def partial(h, t, away, end):
         u = 2 * (end * SIDE + away) if t == 0 else 2 * (away * SIDE + end) + 1
-        return chain[table_s[2, u]]
-
-    def sum_first(t, k, m):
+        return chain[h, table_s[2, u]]
+
+    def sum_first(h, t, k, m):
         to = mesh_id(moved(place, 1 - t, k), core)
         return [
             remote(
-                src.at[t, k, m], dst.at[t, k, m], first_sems.at[0, i, t, k, m],
-                first_sems.at[1, i, t, k, m], to,
+                src.at[h, t, k, m], dst.at[h, t, k, m], first_sems.at[0, i, h, t, k, m],
+                first_sems.at[1, i, h, t, k, m], to,
             )
             for i, (src, dst) in enumerate(((part_u, first_u), (part_q, first_q)))
         ]
 
-    def sum_second(t, m):
+    def sum_second(h, t, m):
         to = mesh_id(moved(place, t, m), core)
         return [
             remote(
-                src.at[t, m], dst.at[t, m], second_sems.at[0, i, t, m],
-                second_sems.at[1, i, t, m], to,
+                src.at[h, t, m], dst.at[h, t, m], second_sems.at[0, i, h, t, m],
+                second_sems.at[1, i, h, t, m], to,
             )
             for i, (src, dst) in enumerate(((sum_u, second_u), (sum_q, second_q)))
         ]
 
     turns = tuple(range(1, SIDE)) + (0,)
 
-    def reduce_start():
+    def reduce_begin(h):
         for m in turns:
             for k in range(1, SIDE):
                 for t in range(2):
                     whole, unit = quantize(
-                        partial(t, (near[t] + k) % SIDE, (far[t] + m) % SIDE)
+                        partial(h, t, (near[t] + k) % SIDE, (far[t] + m) % SIDE)
                     )
-                    part_q[t, k, m] = whole
-                    part_u[t, k, m] = unit
-                    for copy in sum_first(t, k, m):
+                    part_q[h, t, k, m] = whole
+                    part_u[h, t, k, m] = unit
+                    for copy in sum_first(h, t, k, m):
                         copy.start()
 
-    def reduce_finish():
+    def reduce_onward(h):
         for m in turns:
             for t in range(2):
-                total = partial(t, near[t], (far[t] + m) % SIDE)
+                total = partial(h, t, near[t], (far[t] + m) % SIDE)
                 for k in range(1, SIDE):
-                    for copy in sum_first(t, k, m):
+                    for copy in sum_first(h, t, k, m):
                         copy.wait()
-                    total = total + restore(first_q[t, k, m], first_u[t, k, m])
+                    total = total + restore(first_q[h, t, k, m], first_u[h, t, k, m])
                 if m == 0:
-                    sums[t] = total
+                    sums[h, t] = total
                 else:
                     whole, unit = quantize(total)
-                    sum_q[t, m] = whole
-                    sum_u[t, m] = unit
-                    for copy in sum_second(t, m):
+                    sum_q[h, t, m] = whole
+                    sum_u[h, t, m] = unit
+                    for copy in sum_second(h, t, m):
                         copy.start()
+
+    def reduce_end(h):
         totals = []
         for t in range(2):
-            total = sums[t]
+            total = sums[h, t]
             for m in range(1, SIDE):
-                for copy in sum_second(t, m):
+                for copy in sum_second(h, t, m):
                     copy.wait()
-                total = total + restore(second_q[t, m], second_u[t, m])
+                total = total + restore(second_q[h, t, m], second_u[h, t, m])
             totals.append(total)
         return jnp.concatenate(totals, axis=0)
 
@@ -505,35 +533,62 @@
     def row_sum(left, right):
         return jnp.sum(left * right, axis=1, keepdims=True)
 
-    accumulate(True)
-    reduce_start()
-    local[...] = gram_term(prior[...])
-    start = reduce_finish() - local[...]
-    residual[...] = start
-    direction[...] = start
+    norms = []
     out[...] = prior[...]
-
-    def iterate(step, norm_now):
-        d_low = direction[...].astype(jnp.bfloat16)
-        low[y * SIDE + x] = d_low[:tile]
-        low[PLANE + x * SIDE + y] = d_low[tile:]
-        gather_begin()
-        local[...] = gram_term(direction[...])
-        gather_onward()
-        gather_end()
-        accumulate(False)
-        reduce_start()
-        image = local[...] + reduce_finish()
-        d = direction[...]
-        alpha = norm_now / (row_sum(d, image) + EPS)
-        out[...] = out[...] + alpha * d
-        r = residual[...] - alpha * image
-        residual[...] = r
-        fresh = row_sum(r, r)
-        direction[...] = r + fresh / (norm_now + EPS) * d
-        return fresh
-
-    lax.fori_loop(0, ITERS, iterate, row_sum(start, start))
+    for h in range(2):
+        accumulate(h, True)
+        reduce_begin(h)
+    for h in range(2):
+        local[h] = gram_term(half_rows(prior, h))
+    for h in range(2):
+        reduce_onward(h)
+    for h in range(2):
+        start = reduce_end(h) - local[h]
+        residual[h] = start
+        direction[h] = start
+        norms.append(row_sum(start, start))
+        lower(h, start)
+        gather_begin(h)
+    for h in range(2):
+        gather_onward(h)
+        local[h] = gram_term(direction[h])
+
+    def iterate(step, norms):
+        for h in range(2):
+            gather_end(h)
+            accumulate(h, False)
+            reduce_begin(h)
+        for h in range(2):
+            reduce_onward(h)
+        fresh = []
+        for h in range(2):
+            image = local[h] + reduce_end(h)
+            d = direction[h]
+            alpha = norms[h] / (row_sum(d, image) + EPS)
+            for t in range(2):
+                rows = slice(t * tile + h * half, t * tile + (h + 1) * half)
+                block = slice(t * half, (t + 1) * half)
+                out[rows] = out[rows] + alpha[block] * d[block]
+            r = residual[h] - alpha * image
+            residual[h] = r
+            fresh.append(row_sum(r, r))
+            after = r + fresh[h] / (norms[h] + EPS) * d
+            direction[h] = after
+
+            @pl.when(step < ITERS - 1)
+            def _():
+                lower(h, after)
+                gather_begin(h)
+
+        @pl.when(step < ITERS - 1)
+        def _():
+            for h in range(2):
+                gather_onward(h)
+                local[h] = gram_term(direction[h])
+
+        return tuple(fresh)
+
+    lax.fori_loop(0, ITERS, iterate, tuple(norms))
 
 
 def body(user_prior, item_factors, user_tiles, item_tiles, counts):
@@ -545,6 +600,7 @@
     users = 2 * n_grp
     own = user_prior.shape[0]
     held = item_factors.shape[0] // tile
+    half = tile // 2
     grows = rank // n_grp
     vmem = pl.BlockSpec(memory_space=pltpu.VMEM)
     smem = pl.BlockSpec(memory_space=pltpu.SMEM)
@@ -569,33 +625,34 @@
             pltpu.VMEM((pairs, tile, tile), jnp.int32),
             pltpu.VMEM((pairs, tile, tile), low_type),
             pltpu.VMEM((pairs, tile, tile), low_type),
-            pltpu.VMEM((pairs, tile, tile), low_type),
-            pltpu.VMEM((users, tile, rank), low_type),
-            pltpu.VMEM((pairs + 1, tile, rank), full),
+            pltpu.VMEM((pairs, half, tile), low_type),
+            pltpu.VMEM((users, half, rank), low_type),
+            pltpu.VMEM((users, half, rank), low_type),
+            pltpu.VMEM((2, pairs + 1, half, rank), full),
             pltpu.VMEM((n_grp, grows, rank), full),
             pltpu.VMEM((n_grp, grows, rank), full),
             pltpu.VMEM((n_blk, grows, rank), full),
             pltpu.VMEM((n_grp, grows, rank), full),
             pltpu.VMEM((2, grows, rank), full),
-            pltpu.VMEM((2, SIDE, SIDE, tile, rank), whole_type),
-            pltpu.VMEM((2, SIDE, SIDE, 1, rank), full),
-            pltpu.VMEM((2, SIDE, SIDE, tile, rank), whole_type),
-            pltpu.VMEM((2, SIDE, SIDE, 1, rank), full),
-            pltpu.VMEM((2, SIDE, tile, rank), whole_type),
-            pltpu.VMEM((2, SIDE, 1, rank), full),
-            pltpu.VMEM((2, SIDE, tile, rank), whole_type),
-            pltpu.VMEM((2, SIDE, 1, rank), full),
+            pltpu.VMEM((2, 2, SIDE, SIDE, half, rank), whole_type),
+            pltpu.VMEM((2, 2, SIDE, SIDE, 1, rank), full),
+            pltpu.VMEM((2, 2, SIDE, SIDE, half, rank), whole_type),
+            pltpu.VMEM((2, 2, SIDE, SIDE, 1, rank), full),
+            pltpu.VMEM((2, 2, SIDE, half, rank), whole_type),
+            pltpu.VMEM((2, 2, SIDE, 1, rank), full),
+            pltpu.VMEM((2, 2, SIDE, half, rank), whole_type),
+            pltpu.VMEM((2, 2, SIDE, 1, rank), full),
+            pltpu.VMEM((2, 2, half, rank), full),
             pltpu.VMEM((2, tile, rank), full),
-            pltpu.VMEM((own, rank), full),
-            pltpu.VMEM((own, rank), full),
-            pltpu.VMEM((own, rank), full),
-            dma((2, n_all)),
+            pltpu.VMEM((2, tile, rank), full),
+            pltpu.VMEM((2, tile, rank), full),
+            dma((2, PEERS + 1)),
             dma((2, 3, 4)),
             dma((2, 2, 3, FACE)),
-            dma((2, 2, SIDE)),
-            dma((2, 2, SIDE, SIDE)),
+            dma((2, 2, 2, SIDE)),
             dma((2, 2, 2, SIDE, SIDE)),
-            dma((2, 2, 2, SIDE)),
+            dma((2, 2, 2, 2, SIDE, SIDE)),
+            dma((2, 2, 2, 2, SIDE)),
             dma((3, 2, n_grp)),
             dma((3,)),
         ],

time: 232 us -> 205 us (0.88)
  the two profiles are of different devices: /device:TPU:32 before, /device:TPU:0 now
where the time goes in v4:
time: 205 us
  Pallas kernels  203 us (99%)
    pallas_call x1, Pallas kernels, body(): pl.pallas_call(functools.partial(kernel, n_blk, n_grp), out_shape=jax.Sha...  203 us

profile of v4, /device:TPU:0, one launch (start us, length us, event | category | flops | bytes accessed | tf_op | source)
XLA Modules:
  0.0 204.8 jit_solution(2127220333970803505)
XLA Ops:
  0.0 203.2 %als.1 = f32[256,128]{1,0:T(8,128)} custom-call(s32[64]{0:T(128)} %wanted_tiles.1, s32[64]{0:T(128)} %user_tiles.1, bf16[32,128,128]{2,1,0:T(8,128)(2,1)} %bitcast.1, f32[256,128]{1,0:T(8,128)} %prior.1, s32[64,128,128]{2,1,0:T(8,128)} %counts.1), custom_call_target="tpu_custom_call" | custom-call | tf_op jit(solution)/shard_map/als/pallas_call | solution.py:609
  203.3 1.6 copy.7

commit v5 on v4

--- a/solution.py
+++ b/solution.py
@@ -422,7 +422,7 @@
 
     group = 8
 
-    def accumulate(h, with_rhs):
+    def score_all(h):
         part = slice(h * half, (h + 1) * half)
 
         def score(i, carry):
@@ -436,6 +436,9 @@
             return carry
 
         lax.fori_loop(0, pairs // group, score, 0)
+
+    def spread_all(h, with_rhs):
+        part = slice(h * half, (h + 1) * half)
 
         def spread(i, carry):
             backs = []
@@ -533,35 +536,48 @@
     def row_sum(left, right):
         return jnp.sum(left * right, axis=1, keepdims=True)
 
+    def products(with_rhs):
+        score_all(0)
+        if not with_rhs:
+            gather_onward(1)
+        spread_all(0, with_rhs)
+        reduce_begin(0)
+        if not with_rhs:
+            gather_end(1)
+        score_all(1)
+        reduce_onward(0)
+        spread_all(1, with_rhs)
+        reduce_begin(1)
+
+    def launch(h, vectors):
+        lower(h, vectors)
+        gather_begin(h)
+        local[h] = gram_term(vectors)
+
     norms = []
     out[...] = prior[...]
     for h in range(2):
-        accumulate(h, True)
-        reduce_begin(h)
+        local[h] = gram_term(half_rows(prior, h))
+    products(True)
     for h in range(2):
-        local[h] = gram_term(half_rows(prior, h))
-    for h in range(2):
-        reduce_onward(h)
-    for h in range(2):
+        if h == 1:
+            reduce_onward(1)
+            gather_onward(0)
         start = reduce_end(h) - local[h]
         residual[h] = start
         direction[h] = start
         norms.append(row_sum(start, start))
-        lower(h, start)
-        gather_begin(h)
-    for h in range(2):
-        gather_onward(h)
-        local[h] = gram_term(direction[h])
+        launch(h, start)
 
     def iterate(step, norms):
-        for h in range(2):
-            gather_end(h)
-            accumulate(h, False)
-            reduce_begin(h)
-        for h in range(2):
-            reduce_onward(h)
+        more = step < ITERS - 1
+        gather_end(0)
+        products(False)
         fresh = []
         for h in range(2):
+            if h == 1:
+                reduce_onward(1)
+                pl.when(more)(functools.partial(gather_onward, 0))
             image = local[h] + reduce_end(h)
             d = direction[h]
             alpha = norms[h] / (row_sum(d, image) + EPS)
@@ -574,17 +590,7 @@
             fresh.append(row_sum(r, r))
             after = r + fresh[h] / (norms[h] + EPS) * d
             direction[h] = after
-
-            @pl.when(step < ITERS - 1)
-            def _():
-                lower(h, after)
-                gather_begin(h)
-
-        @pl.when(step < ITERS - 1)
-        def _():
-            for h in range(2):
-                gather_onward(h)
-                local[h] = gram_term(direction[h])
+            pl.when(more)(functools.partial(launch, h, after))
 
         return tuple(fresh)
 

time: 205 us -> 206 us (level)
  no operation moved by 1% of the time
where the time goes in v5:
time: 206 us
  Pallas kernels  204 us (99%)
    pallas_call x1, Pallas kernels, body(): pl.pallas_call(functools.partial(kernel, n_blk, n_grp), out_shape=jax.Sha...  204 us

profile of v5, /device:TPU:0, one launch (start us, length us, event | category | flops | bytes accessed | tf_op | source)
XLA Modules:
  0.0 205.7 jit_solution(15452654457563852464)
XLA Ops:
  0.0 204.2 %als.1 = f32[256,128]{1,0:T(8,128)} custom-call(s32[64]{0:T(128)} %wanted_tiles.1, s32[64]{0:T(128)} %user_tiles.1, bf16[32,128,128]{2,1,0:T(8,128)(2,1)} %bitcast.1, f32[256,128]{1,0:T(8,128)} %prior.1, s32[64,128,128]{2,1,0:T(8,128)} %counts.1), custom_call_target="tpu_custom_call" | custom-call | tf_op jit(solution)/shard_map/als/pallas_call | solution.py:615
  204.2 1.6 copy.7

commit v6 on v5

--- a/solution.py
+++ b/solution.py
@@ -183,45 +183,35 @@
         for axis in range(3):
             ring_copy(axis, kind).start()
 
-    def low_place(t, m):
-        if t == 0:
-            return y * SIDE + (x + SIDE - m) % SIDE
-        return PLANE + x * SIDE + (y + SIDE - m) % SIDE
-
     def gather_a(h, t, k):
-        ref = lows[h].at[low_place(t, 0)]
+        ref = lows[h].at[y * SIDE + x if t == 0 else PLANE + x * SIDE + y]
         return remote(
             ref, ref, gather_one.at[0, h, t, k], gather_one.at[1, h, t, k],
             mesh_id(moved(place, t, k), core),
         )
 
-    def gather_b(h, t, k, m):
-        ref = lows[h].at[low_place(t, m)]
+    def gather_b(h, t, k):
+        ref = lows[h].at[pl.ds(y * SIDE if t == 0 else PLANE + x * SIDE, SIDE)]
         return remote(
-            ref, ref, gather_two.at[0, h, t, k, m], gather_two.at[1, h, t, k, m],
+            ref, ref, gather_two.at[0, h, t, k], gather_two.at[1, h, t, k],
             mesh_id(moved(place, 1 - t, k), core),
         )
 
+    every = [(k, t) for k in (1, 3, 2) for t in range(2)]
+
     def gather_begin(h):
-        for k in range(1, SIDE):
-            for t in range(2):
-                gather_a(h, t, k).start()
-        for k in range(1, SIDE):
-            for t in range(2):
-                gather_b(h, t, k, 0).start()
+        for k, t in every:
+            gather_a(h, t, k).start()
 
     def gather_onward(h):
-        for m in range(1, SIDE):
-            for t in range(2):
-                gather_a(h, t, m).wait()
-                for k in range(1, SIDE):
-                    gather_b(h, t, k, m).start()
+        for k, t in every:
+            gather_a(h, t, k).wait()
+        for k, t in every:
+            gather_b(h, t, k).start()
 
     def gather_end(h):
-        for m in range(SIDE):
-            for k in range(1, SIDE):
-                for t in range(2):
-                    gather_b(h, t, k, m).wait()
+        for k, t in every:
+            gather_b(h, t, k).wait()
 
     gather_begin(0)
     gather_begin(1)
@@ -464,12 +454,12 @@
         u = 2 * (end * SIDE + away) if t == 0 else 2 * (away * SIDE + end) + 1
         return chain[h, table_s[2, u]]
 
-    def sum_first(h, t, k, m):
+    def sum_first(h, t, k):
         to = mesh_id(moved(place, 1 - t, k), core)
         return [
             remote(
-                src.at[h, t, k, m], dst.at[h, t, k, m], first_sems.at[0, i, h, t, k, m],
-                first_sems.at[1, i, h, t, k, m], to,
+                src.at[h, t, k], dst.at[h, t, k], first_sems.at[0, i, h, t, k],
+                first_sems.at[1, i, h, t, k], to,
             )
             for i, (src, dst) in enumerate(((part_u, first_u), (part_q, first_q)))
         ]
@@ -484,27 +474,25 @@
             for i, (src, dst) in enumerate(((sum_u, second_u), (sum_q, second_q)))
         ]
 
-    turns = tuple(range(1, SIDE)) + (0,)
-
     def reduce_begin(h):
-        for m in turns:
-            for k in range(1, SIDE):
-                for t in range(2):
-                    whole, unit = quantize(
-                        partial(h, t, (near[t] + k) % SIDE, (far[t] + m) % SIDE)
-                    )
-                    part_q[h, t, k, m] = whole
-                    part_u[h, t, k, m] = unit
-                    for copy in sum_first(h, t, k, m):
-                        copy.start()
+        for k, t in every:
+            for m in range(SIDE):
+                whole, unit = quantize(
+                    partial(h, t, (near[t] + k) % SIDE, (far[t] + m) % SIDE)
+                )
+                part_q[h, t, k, m] = whole
+                part_u[h, t, k, m] = unit
+            for copy in sum_first(h, t, k):
+                copy.start()
 
     def reduce_onward(h):
-        for m in turns:
+        for k, t in every:
+            for copy in sum_first(h, t, k):
+                copy.wait()
+        for m in (1, 3, 2, 0):
             for t in range(2):
                 total = partial(h, t, near[t], (far[t] + m) % SIDE)
                 for k in range(1, SIDE):
-                    for copy in sum_first(h, t, k, m):
-                        copy.wait()
                     total = total + restore(first_q[h, t, k, m], first_u[h, t, k, m])
                 if m == 0:
                     sums[h, t] = total
@@ -656,8 +644,8 @@
             dma((2, 3, 4)),
             dma((2, 2, 3, FACE)),
             dma((2, 2, 2, SIDE)),
-            dma((2, 2, 2, SIDE, SIDE)),
-            dma((2, 2, 2, 2, SIDE, SIDE)),
+            dma((2, 2, 2, SIDE)),
+            dma((2, 2, 2, 2, SIDE)),
             dma((2, 2, 2, 2, SIDE)),
             dma((3, 2, n_grp)),
             dma((3,)),

time: 206 us -> 211 us (1.024)
  Pallas kernels: 204 us -> 209 us
    pallas_call x1, Pallas kernels: 204 us -> 209 us  [body(): pl.pallas_call(functools.partial(kernel, n_blk, n_grp), out_shape=jax.Sha...]
where the time goes in v6:
time: 211 us
  Pallas kernels  209 us (99%)
    pallas_call x1, Pallas kernels, body(): pl.pallas_call(functools.partial(kernel, n_blk, n_grp), out_shape=jax.Sha...  209 us

profile of v6, /device:TPU:0, one launch (start us, length us, event | category | flops | bytes accessed | tf_op | source)
XLA Modules:
  0.0 210.6 jit_solution(17221000090725456325)
XLA Ops:
  0.0 209.0 %als.1 = f32[256,128]{1,0:T(8,128)} custom-call(s32[64]{0:T(128)} %wanted_tiles.1, s32[64]{0:T(128)} %user_tiles.1, bf16[32,128,128]{2,1,0:T(8,128)(2,1)} %bitcast.1, f32[256,128]{1,0:T(8,128)} %prior.1, s32[64,128,128]{2,1,0:T(8,128)} %counts.1), custom_call_target="tpu_custom_call" | custom-call | tf_op jit(solution)/shard_map/als/pallas_call | solution.py:603
  209.0 1.6 copy.7

commit v7 on v5

--- a/solution.py
+++ b/solution.py
@@ -15,6 +15,7 @@
 PLANE = SIDE * SIDE
 FACE = 2 * PLANE
 PEERS = 73
+SLOTS = 2 * SIDE
 LEVELS = 32700.0
 SHARE = ((0, 48), (48, 48), (96, 32))
 AROUND = (0, 1, 3, 2)
@@ -292,7 +293,7 @@
             w = (place[axis] + AROUND[i]) % SIDE
             pair = want[to, 0, flat_id(put_at(place, axis, w), core)]
             for j, held_at in enumerate((pair % 256, pair // 256)):
-                ref[slot, i, j] = rings[axis][i, held_at] if i < CLOSE else fars[axis][held_at]
+                ref[slot * SLOTS + 2 * i + j] = rings[axis][i, held_at] if i < CLOSE else fars[axis][held_at]
 
     levels = (tuple(range(CLOSE)), tuple(range(CLOSE, SIDE)))
 
@@ -303,9 +304,10 @@
 
     def parcel(level, axis, step):
         to, to_core = face_target(axis, step)
-        part = pl.ds(levels[level][0], len(levels[level]))
+        start, size = 2 * levels[level][0], 2 * len(levels[level])
         return remote(
-            sends[axis].at[step, part], recvs[axis].at[face_index(axis), part],
+            sends[axis].at[pl.ds(step * SLOTS + start, size)],
+            recvs[axis].at[pl.ds(face_index(axis) * SLOTS + start, size)],
             tile_sems.at[0, level, axis, step], tile_sems.at[1, level, axis, step],
             mesh_id(to, to_core),
         )
@@ -359,7 +361,7 @@
         pack_into(recvs[axis], face_index(axis), axis, me, range(SIDE))
 
     def link(p, state):
-        seen, order, last, before = state
+        seen, order, last, before, users_of = state
         owner = wanted_tiles[p] // held
         hit = lane == owner
         turn = jnp.sum(jnp.where(hit, seen, 0), axis=1, keepdims=True)
@@ -369,13 +371,22 @@
         earlier = jnp.sum(jnp.where(mine, last, 0), axis=1, keepdims=True)
         before = jnp.where(lane == p, earlier, before)
         last = jnp.where(mine, p + 1, last)
-        return seen, order, last, before
-
-    _, order, last, before = lax.fori_loop(0, pairs, link, (zero,) * 4)
-    row = lax.broadcasted_iota(jnp.int32, (8, 128), 0)
-    table[...] = jnp.where(
-        row == 0, order, jnp.where(row == 1, before, jnp.where(row == 2, last, 0))
-    )
+        users_of = jnp.where(lane == p, user_tiles[p], users_of)
+        return seen, order, last, before, users_of
+
+    _, order, last, before, users_of = lax.fori_loop(0, pairs, link, (zero,) * 5)
+    owner = order // 2
+    owner_b, owner_g = owner // n_grp, owner % n_grp
+    at, of = (owner_g // SIDE, owner_g % SIDE, owner_b // 2), owner_b % 2
+    table[...] = jnp.zeros((8, 128), jnp.int32)
+    table[1:2] = before
+    table[2:3] = last
+    table[3:4] = tile_place(users_of)
+    for axis in range(3):
+        face = (at[(axis + 1) % 3] * SIDE + at[(axis + 2) % 3]) * 2 + of
+        ahead = (at[axis] + SIDE - place[axis]) % SIDE
+        ahead = jnp.where(ahead >= 2, 5 - ahead, ahead)
+        table[4 + axis:5 + axis] = face * SLOTS + ahead * 2 + order % 2
     table_copy = pltpu.make_async_copy(table, table_s, local_sems.at[2])
     table_copy.start()
     count_copy.wait()
@@ -407,15 +418,8 @@
     def take(i, carry):
         for j in range(4):
             p = i * 4 + j
-            slot = table_s[0, p]
-            owner, turn = slot // 2, slot % 2
-            ob, og = owner // n_grp, owner % n_grp
-            at, of = (og // SIDE, og % SIDE, ob // 2), ob % 2
             for axis, (start, rows) in enumerate(SHARE):
-                face = (at[(axis + 1) % 3] * SIDE + at[(axis + 2) % 3]) * 2 + of
-                ahead = (at[axis] + SIDE - place[axis]) % SIDE
-                ahead = jnp.where(ahead >= 2, 5 - ahead, ahead)
-                tiles[p, start:start + rows] = recvs[axis][face, ahead, turn]
+                tiles[p, start:start + rows] = recvs[axis][table_s[4 + axis, p]]
         return carry
 
     lax.fori_loop(0, pairs // 4, take, 0)
@@ -429,34 +433,57 @@
             for j in range(group):
                 p = i * group + j
                 scores = lax.dot_general(
-                    lows[h][tile_place(user_tiles[p])], tiles[p], (((1,), (1,)), ((), ())),
+                    lows[h][table_s[3, p]], tiles[p], (((1,), (1,)), ((), ())),
                     preferred_element_type=jnp.float32,
                 )
-                scaled[p] = (weights[p, part].astype(jnp.float32) * scores).astype(jnp.bfloat16)
+                scaled[p, :half] = (weights[p, part].astype(jnp.float32) * scores).astype(jnp.bfloat16)
             return carry
 
         lax.fori_loop(0, pairs // group, score, 0)
 
-    def spread_all(h, with_rhs):
-        part = slice(h * half, (h + 1) * half)
-
+    def spread_all(h):
         def spread(i, carry):
-            backs = []
-            for j in range(group):
-                p = i * group + j
-                back = jnp.dot(scaled[p], tiles[p], preferred_element_type=jnp.float32)
-                if with_rhs:
-                    pulled = jnp.dot(
-                        pulls[p, part], tiles[p], preferred_element_type=jnp.float32
-                    )
-                    back = pulled - back
-                backs.append(back)
+            backs = [
+                jnp.dot(scaled[p, :half], tiles[p], preferred_element_type=jnp.float32)
+                for p in (i * group + j for j in range(group))
+            ]
             for j in range(group):
                 p = i * group + j
                 chain[h, p + 1] = chain[h, table_s[1, p]] + backs[j]
             return carry
 
         lax.fori_loop(0, pairs // group, spread, 0)
+
+    def first_products():
+        def score(i, carry):
+            for j in range(group):
+                p = i * group + j
+                at = table_s[3, p]
+                scores = lax.dot_general(
+                    jnp.concatenate([lows[0][at], lows[1][at]], axis=0), tiles[p],
+                    (((1,), (1,)), ((), ())), preferred_element_type=jnp.float32,
+                )
+                scaled[p] = (weights[p].astype(jnp.float32) * scores).astype(jnp.bfloat16)
+            return carry
+
+        lax.fori_loop(0, pairs // group, score, 0)
+
+        def spread(i, carry):
+            backs = []
+            for j in range(group // 2):
+                p = i * (group // 2) + j
+                backs.append(
+                    jnp.dot(pulls[p], tiles[p], preferred_element_type=jnp.float32)
+                    - jnp.dot(scaled[p], tiles[p], preferred_element_type=jnp.float32)
+                )
+            for j in range(group // 2):
+                p = i * (group // 2) + j
+                for h in range(2):
+                    part = backs[j][h * half:(h + 1) * half]
+                    chain[h, p + 1] = chain[h, table_s[1, p]] + part
+            return carry
+
+        lax.fori_loop(0, pairs // (group // 2), spread, 0)
 
     near, far = (y, x), (x, y)
 
@@ -536,17 +563,15 @@
     def row_sum(left, right):
         return jnp.sum(left * right, axis=1, keepdims=True)
 
-    def products(with_rhs):
+    def products():
         score_all(0)
-        if not with_rhs:
-            gather_onward(1)
-        spread_all(0, with_rhs)
+        gather_onward(1)
+        spread_all(0)
         reduce_begin(0)
-        if not with_rhs:
-            gather_end(1)
+        gather_end(1)
         score_all(1)
         reduce_onward(0)
-        spread_all(1, with_rhs)
+        spread_all(1)
         reduce_begin(1)
 
     def launch(h, vectors):
@@ -556,9 +581,12 @@
 
     norms = []
     out[...] = prior[...]
+    first_products()
+    for h in range(2):
+        reduce_begin(h)
     for h in range(2):
         local[h] = gram_term(half_rows(prior, h))
-    products(True)
+    reduce_onward(0)
     for h in range(2):
         if h == 1:
             reduce_onward(1)
@@ -572,7 +600,7 @@
     def iterate(step, norms):
         more = step < ITERS - 1
         gather_end(0)
-        products(False)
+        products()
         fresh = []
         for h in range(2):
             if h == 1:
@@ -625,13 +653,13 @@
             pltpu.SMEM((8, 128), jnp.int32),
             *(pltpu.VMEM((CLOSE, held, rows, rank), low_type) for _, rows in SHARE),
             *(pltpu.VMEM((held, rows, rank), low_type) for _, rows in SHARE),
-            *(pltpu.VMEM((FACE, SIDE, 2, rows, rank), low_type) for _, rows in SHARE),
-            *(pltpu.VMEM((FACE, SIDE, 2, rows, rank), low_type) for _, rows in SHARE),
+            *(pltpu.VMEM((FACE * SLOTS, rows, rank), low_type) for _, rows in SHARE),
+            *(pltpu.VMEM((FACE * SLOTS, rows, rank), low_type) for _, rows in SHARE),
             pltpu.VMEM((pairs, tile, rank), low_type),
             pltpu.VMEM((pairs, tile, tile), jnp.int32),
             pltpu.VMEM((pairs, tile, tile), low_type),
             pltpu.VMEM((pairs, tile, tile), low_type),
-            pltpu.VMEM((pairs, half, tile), low_type),
+            pltpu.VMEM((pairs, tile, tile), low_type),
             pltpu.VMEM((users, half, rank), low_type),
             pltpu.VMEM((users, half, rank), low_type),
             pltpu.VMEM((2, pairs + 1, half, rank), full),

time: 206 us -> 203 us (0.985)
    pallas_call x1, Pallas kernels: 204 us -> 202 us  [body(): pl.pallas_call(functools.partial(kernel, n_blk, n_grp), out_shape=jax.Sha...]
where the time goes in v7:
time: 203 us
  Pallas kernels  202 us (100%)
    pallas_call x1, Pallas kernels, body(): pl.pallas_call(functools.partial(kernel, n_blk, n_grp), out_shape=jax.Sha...  202 us

profile of v7, /device:TPU:0, one launch (start us, length us, event | category | flops | bytes accessed | tf_op | source)
XLA Modules:
  0.0 203.3 jit_solution(8000990770579999077)
XLA Ops:
  0.0 201.8 %als.1 = f32[256,128]{1,0:T(8,128)} custom-call(s32[64]{0:T(128)} %wanted_tiles.1, s32[64]{0:T(128)} %user_tiles.1, bf16[32,128,128]{2,1,0:T(8,128)(2,1)} %bitcast.1, f32[256,128]{1,0:T(8,128)} %prior.1, s32[64,128,128]{2,1,0:T(8,128)} %counts.1), custom_call_target="tpu_custom_call" | custom-call | tf_op jit(solution)/shard_map/als/pallas_call | solution.py:643
  201.8 1.6 copy.7

commit v8 on v7

--- a/solution.py
+++ b/solution.py
@@ -109,24 +109,19 @@
     count_copy = pltpu.make_async_copy(counts, counted, local_sems.at[0])
     count_copy.start()
 
-    def same_x(i):
-        return (place[0], (y + i // 8) % SIDE, (z + i // 2) % SIDE), (core + i) % 2
-
-    def same_y(i):
-        return ((x + 1 + i // 8) % SIDE, place[1], (z + i // 2) % SIDE), (core + i) % 2
-
-    def same_z(i):
-        return ((x + 1 + i // 2 % 3) % SIDE, (y + 1 + i // 6) % SIDE, place[2]), (core + i) % 2
-
-    families = ((same_x, 1, 32, 0), (same_y, 0, 24, 32), (same_z, 0, 18, 56))
+    xs, ys, zs = ([(v + d) % SIDE for d in range(SIDE)] for v in place)
+    planes = [[xs[i] * SIDE + ys[j] for j in range(SIDE)] for i in range(SIDE)]
+    stacks = [[zs[k] * 2 + c for c in (core, 1 - core)] for k in range(SIDE)]
+    peers = [
+        (stacks[k][c], planes[i][j])
+        for i in range(SIDE) for j in range(SIDE) for k in range(SIDE) for c in range(2)
+        if i * j * k == 0 and i + j + k + c > 0
+    ]
+    assert len(peers) == PEERS
 
     def for_peers(act):
-        for family, first, last, base in families:
-            def one(i, carry):
-                act(mesh_id(*family(i)), base + i)
-                return carry
-
-            lax.fori_loop(first, last, one, 0)
+        for i, to in enumerate(peers):
+            act(to, i)
 
     barrier = pltpu.get_barrier_semaphore()
     for_peers(
@@ -151,13 +146,6 @@
     reqs[me] = asked
     for h in range(2):
         lower(h, half_rows(prior, h))
-
-    def keep(i, carry):
-        for axis, (start, rows) in enumerate(SHARE):
-            rings[axis][0, i] = items[i, start:start + rows]
-        return carry
-
-    lax.fori_loop(0, held, keep, 0)
 
     pl.semaphore_wait(barrier, PEERS)
 
@@ -226,6 +214,13 @@
 
     gather_begin(0)
     gather_begin(1)
+
+    def keep(i, carry):
+        for axis, (start, rows) in enumerate(SHARE):
+            rings[axis][0, i] = items[i, start:start + rows]
+        return carry
+
+    lax.fori_loop(0, held, keep, 0)
 
     chunk = min(8, held)
 
@@ -680,7 +675,7 @@
             pltpu.VMEM((2, tile, rank), full),
             pltpu.VMEM((2, tile, rank), full),
             pltpu.VMEM((2, tile, rank), full),
-            dma((2, PEERS + 1)),
+            dma((2, PEERS)),
             dma((2, 3, 4)),
             dma((2, 2, 3, FACE)),
             dma((2, 2, 2, SIDE)),

time: 203 us -> 202 us (level)
  no operation moved by 1% of the time
where the time goes in v8:
time: 202 us
  Pallas kernels  200 us (99%)
    pallas_call x1, Pallas kernels, body(): pl.pallas_call(functools.partial(kernel, n_blk, n_grp), out_shape=jax.Sha...  200 us

profile of v8, /device:TPU:0, one launch (start us, length us, event | category | flops | bytes accessed | tf_op | source)
XLA Modules:
  0.0 201.6 jit_solution(11460645550452374628)
XLA Ops:
  0.0 200.0 %als.1 = f32[256,128]{1,0:T(8,128)} custom-call(s32[64]{0:T(128)} %wanted_tiles.1, s32[64]{0:T(128)} %user_tiles.1, bf16[32,128,128]{2,1,0:T(8,128)(2,1)} %bitcast.1, f32[256,128]{1,0:T(8,128)} %prior.1, s32[64,128,128]{2,1,0:T(8,128)} %counts.1), custom_call_target="tpu_custom_call" | custom-call | tf_op jit(solution)/shard_map/als/pallas_call | solution.py:638
  200.0 1.6 copy.7
